TPU v7x, 768 devices: a whole 4x8x12 slice. The times are simulated.
768 devices in a mesh: tensor: 48 (over y_hi, z), context: 16 (over x, y_lo, core).
Axes of the slice: x: 4, y: 8 (y_hi: 4, y_lo: 2; y = y_hi * 2 + y_lo), z: 12, core: 2. Of those that a mesh axis runs over, the one named last changes fastest.
Arguments:
- tokens: bfloat16 [6144, 8192], P('context'), may hold values from -48 to 48
- w_query: bfloat16 [8192, 6144], P(None, 'tensor'), may hold values from -0.0625 to 0.0625
- w_key: bfloat16 [8192, 6144], P(None, 'tensor'), may hold values from -0.0625 to 0.0625
- w_value: bfloat16 [8192, 6144], P(None, 'tensor'), may hold values from -0.0625 to 0.0625
- mix_gate: bfloat16 [48, 96], replicated, may hold values from -0.875 to 0.875
- mix_up: bfloat16 [48, 96], replicated, may hold values from -0.875 to 0.875
- mix_down: bfloat16 [96, 48], replicated, may hold values from -0.625 to 0.625
- block_ids: int32 [64], P('context'), may hold values from 0 to 31, as said below
Outputs:
- attended: bfloat16 [6144, 6144], P('context', 'tensor')
Inputs may be any that keep to these rules, and one draw needn't show every extreme that they name: `block_ids`: device c of the context axis holds entries 4c to 4c+3: (a, 31 - a) for the first sequence and (b, 31 - b) for the second; over all devices each sequence's block numbers appear once each.
All inputs are finite; a program needn't handle non-finite values.
Results may differ from a plain program's by a relative error of at most 0.012.
The roundings to bfloat16 on the way count: a program that leaves them out, or rounds other values in their place, can miss the bound.
Values may be sent and summed in bfloat16 or wider, within the bound.
No kernel may reach another device: no remote copies, remote signals or barrier semaphores. Data moves between devices by JAX's collectives and lax.ppermute only.
A program may use at most 64 MiB of HBM per device.

v0:
```python
import jax
import jax.numpy as jnp
from jax import lax
from jax.sharding import PartitionSpec as P

HEAD_DIM = 128
BLK = 96


def mix_exchanged(gathered, mix_gate, mix_up, mix_down):
    gate_part = jnp.einsum("hnc,hf->ncf", gathered, mix_gate, preferred_element_type=jnp.float32)
    up_part = jnp.einsum("hnc,hf->ncf", gathered, mix_up, preferred_element_type=jnp.float32)
    hidden = (jax.nn.silu(gate_part) * up_part).astype(jnp.bfloat16)
    mixing = jnp.einsum("ncf,fh->hnc", hidden, mix_down, preferred_element_type=jnp.float32)
    return (gathered.astype(jnp.float32) + mixing).astype(jnp.bfloat16)


def shards(tokens, w_query, w_key, w_value, mix_gate, mix_up, mix_down, block_ids):
    query_rows = jnp.dot(tokens, w_query, preferred_element_type=jnp.float32).astype(jnp.bfloat16)
    key_rows = jnp.dot(tokens, w_key, preferred_element_type=jnp.float32).astype(jnp.bfloat16)
    value_rows = jnp.dot(tokens, w_value, preferred_element_type=jnp.float32).astype(jnp.bfloat16)
    local_count = tokens.shape[0]
    local_offsets = jnp.arange(local_count, dtype=jnp.int32)
    query_pos = (
        jnp.repeat(block_ids, BLK, total_repeat_length=local_count) * BLK + local_offsets % BLK
    )
    query_seq = local_offsets // BLK % 4 // 2
    block_all = lax.all_gather(block_ids, "context", axis=0, tiled=True)
    mixed_here = mix_exchanged(
        lax.all_to_all(value_rows[None], "tensor", split_axis=1, concat_axis=0, tiled=True),
        mix_gate,
        mix_up,
        mix_down,
    )
    mixed_rows = lax.all_to_all(mixed_here, "tensor", split_axis=0, concat_axis=1, tiled=True)[0]
    scale = HEAD_DIM ** (-0.5)
    running_max = jnp.full((local_count,), -1e30, jnp.float32)
    running_total = jnp.zeros((local_count,), jnp.float32)
    running_sum = jnp.zeros((local_count, query_rows.shape[1]), jnp.float32)
    key_piece = lax.all_gather(key_rows, "context", axis=0, tiled=True)
    value_piece = lax.all_gather(mixed_rows, "context", axis=0, tiled=True)
    count = key_piece.shape[0]
    offsets = jnp.arange(count, dtype=jnp.int32)
    key_pos = jnp.repeat(block_all, BLK, total_repeat_length=count) * BLK + offsets % BLK
    key_seq = offsets // BLK % 4 // 2
    allowed = (query_seq[:, None] == key_seq[None, :]) & (key_pos[None, :] <= query_pos[:, None])
    scores = (
        lax.dot_general(
            query_rows, key_piece, (((1,), (1,)), ((), ())), preferred_element_type=jnp.float32
        )
        * scale
    )
    scores = jnp.where(allowed, scores, -1e30)
    new_max = jnp.maximum(running_max, jnp.max(scores, axis=1))
    correction = jnp.exp(running_max - new_max)
    weights = jnp.where(allowed, jnp.exp(scores - new_max[:, None]), 0.0)
    new_total = running_total * correction + jnp.sum(weights, axis=1)
    new_sum = running_sum * correction[:, None] + jnp.dot(
        weights.astype(jnp.bfloat16), value_piece, preferred_element_type=jnp.float32
    )
    return (new_sum / new_total[:, None]).astype(jnp.bfloat16)


def solution(mesh):
    in_specs = (
        P("context", None),
        P(None, "tensor"),
        P(None, "tensor"),
        P(None, "tensor"),
        P(),
        P(),
        P(),
        P("context"),
    )
    out_specs = P("context", "tensor")
    return jax.shard_map(shards, mesh=mesh, in_specs=in_specs, out_specs=out_specs, check_vma=False)
```

profile of v0, /device:TPU:8, one launch (start us, length us, event | category | flops | bytes accessed | tf_op | source)
XLA Modules:
  0.0 167.6 jit_solution(17868000420279591522)
XLA Ops:
  6.5 6.0 %convolution_convert_fusion.1 = bf16[384,128]{1,0:T(8,128)(2,1)} fusion(bf16[384,8192]{1,0:T(8,128)(2,1)} %param.12, bf16[8192,128]{1,0:T(8,128)(2,1)} %param.14), kind=kOutput, calls=%fused_computation.14 | convolution fusion | flops 805355520 | bytes 8486912 | tf_op jit(solution)/shard_map/dot_general | solution.py:20
  12.5 0.0 all-gather.3.cloned.1.call-update
  12.6 0.0 copy-start.5
  12.6 0.0 copy-start.6
  12.6 0.0 copy-start.7
  12.6 0.0 copy-start.8
  12.6 0.0 copy-start.10
  12.6 0.0 copy-start.11
  12.6 0.0 copy-start.12
  12.7 0.0 copy-start.13
  12.7 0.0 copy-start.14
  12.7 0.0 copy-start.15
  12.7 0.0 copy-start.17
  12.7 0.0 copy-start.18
  12.7 0.0 copy-start.19
  12.7 0.0 copy-start.20
  12.8 0.0 copy-start.21
  12.8 0.0 copy-start.22
  12.8 0.0 copy-start.24
  12.8 0.0 copy-start.25
  12.8 0.0 copy-start.26
  12.8 0.0 copy-start.27
  12.9 0.0 copy-start.29
  12.9 0.0 copy-start.30
  12.9 0.0 copy-start.31
  12.9 0.0 copy-start.32
  12.9 0.0 copy-start.33
  12.9 0.0 copy-start.34
  12.9 0.0 copy-start.36
  13.0 0.0 copy-start.37
  13.0 0.0 copy-start.38
  13.0 0.0 copy-start.39
  13.0 0.0 copy-start.40
  13.0 5.3 %fusion.12 = bf16[1,384,128]{2,1,0:T(8,128)(2,1)S(1)} fusion(bf16[384,8192]{1,0:T(8,128)(2,1)} %param.12, bf16[8192,128]{1,0:T(8,128)(2,1)} %param.15), kind=kOutput, calls=%fused_computation.16 | convolution fusion | flops 805355520 | bytes 8486912 | tf_op jit(solution)/shard_map/dot_general | solution.py:21
  18.3 0.2 copy.30
  18.5 0.5 broadcast.596
  19.0 1.2 reduce.4
  20.2 0.7 reshape.368
  20.9 20.2 %all-to-all-start = ((bf16[48,2,512]{2,1,0:T(2,128)(2,1)}), bf16[48,2,512]{2,1,0:T(2,128)(2,1)S(1)}, u32[]{:S(2)}, u32[]{:S(2)}) async-start(bf16[48,2,512]{2,1,0:T(2,128)(2,1)} %reshape.368), calls=%async_computation | async-start | bytes 196608 | tf_op jit(solution)/shard_map/all_to_all | solution.py:30
  41.1 1.3 dynamic-slice.12
  42.9 0.2 dynamic-update-slice.6
  43.2 12.2 %all-reduce = s32[64]{0:T(128)S(1)} all-reduce(s32[64]{0:T(128)S(1)} %dynamic-update-slice.6), channel_id=1, replica_groups=mesh['tensor'=48,'context'=16] {'context'}, use_global_device_ids=true, to_apply=%add | all-reduce | flops 64 | bytes 512
  55.4 1.3 all-to-all-done
  56.7 0.1 reshape.369
  56.8 0.2 fusion.25
  57.0 1.1 fusion.11
  58.2 0.7 copy.20
  58.8 13.6 %all-to-all-start.1 = ((bf16[48,8,128]{2,1,0:T(8,128)(2,1)}), bf16[48,8,128]{2,1,0:T(8,128)(2,1)S(1)}, u32[]{:S(2)}, u32[]{:S(2)}) async-start(bf16[48,8,128]{2,1,0:T(8,128)(2,1)} %copy.20), calls=%async_computation.1 | async-start | bytes 196608 | tf_op jit(solution)/shard_map/all_to_all | solution.py:35
  72.4 0.2 all-gather.5.cloned.1.call-start
  72.6 0.7 fusion.62
  73.4 0.7 fusion.59
  74.1 13.9 %all-to-all-done.1 = bf16[48,8,128]{2,1,0:T(8,128)(2,1)S(1)} async-done(((bf16[48,8,128]{2,1,0:T(8,128)(2,1)}), bf16[48,8,128]{2,1,0:T(8,128)(2,1)S(1)}, u32[]{:S(2)}, u32[]{:S(2)}) %all-to-all-start.1) | async-done | bytes 98336 | tf_op jit(solution)/shard_map/all_to_all | solution.py:35
  88.0 0.6 copy-done.1
  88.6 0.0 all-gather.5.cloned.1.call-update
  88.7 0.7 fusion.58
  89.3 0.7 fusion.60
  90.0 0.7 fusion.61
  90.8 3.2 %add_select_fusion.3 = (s32[384]{0:T(512)S(1)}, s32[384]{0:T(512)S(1)}) fusion(pred[384]{0:T(512)(128)(4,1)} %constant.409, pred[384]{0:T(512)(128)(4,1)} %constant.410, pred[384]{0:T(512)(128)(4,1)} %constant.411, s32[]{:T(128)} %bitcast.68, s32[]{:T(128)} %bitcast.67, s32[]{:T(128)} %bitcast.66, s32[]{:T(128)} %bitcast.65), kind=kLoop, calls=%fused_computation.63 | loop fusion | flops 16512 | bytes 4240 | tf_op jit(solution)/shard_map/jit(floor_divide)/jit(_where)/select_n | solution.py:27
  94.3 41.1 %fusion.37 = s32[6144]{0:T(1024)S(1)} fusion(pred[6144]{0:T(1024)(128)(4,1)S(1)} %copy-done.4, pred[6144]{0:T(1024)(128)(4,1)S(1)} %copy-done.5, pred[6144]{0:T(1024)(128)(4,1)S(1)} %copy-done.6, pred[6144]{0:T(1024)(128)(4,1)S(1)} %copy-done.7, pred[6144]{0:T(1024)(128)(4,1)S(1)} %copy-done.8, pred[6144]{0:T(1024)(128)(4,1)S(1)} %copy-done.9, ...), kind=kLoop, calls=%fused_computation.48 | loop fusion | flops 436224 | bytes 411904 | tf_op jit(solution)/shard_map/add | solution.py:44
  135.5 0.0 all-gather.3.cloned.1.call-done
  135.5 12.3 %fusion.63 = (f32[384]{0:T(512)S(1)}, f32[384,6144]{1,0:T(8,128)}) fusion(bf16[6144,128]{1,0:T(8,128)(2,1)} %all-gather.3.cloned.1.call-done, bf16[384,8192]{1,0:T(8,128)(2,1)} %param.12, bf16[8192,128]{1,0:T(8,128)(2,1)S(1)} %copy-done, s32[384]{0:T(512)S(1)} %get-tuple-element.102, s32[6144]{0:T(1024)S(1)} %fusion.37, s32[6144]{0:T(1024)S(1)} %add_select_fusion, ...), kind=kOutput, calls=%fused_computation.90 | convolution fusion | flops 1423490688 | bytes 19452416 | tf_op jit(solution)/shard_map/dot_general | solution.py:48
  147.9 5.7 %fusion = f32[384]{0:T(512)S(1)} fusion(f32[384,6144]{1,0:T(8,128)} %get-tuple-element.100, f32[384]{0:T(512)S(1)} %broadcast_maximum_fusion, s32[6144]{0:T(1024)S(1)} %fusion.37, s32[6144]{0:T(1024)S(1)} %add_select_fusion, s32[384]{0:T(512)S(1)} %get-tuple-element.102, s32[384]{0:T(512)S(1)} %get-tuple-element.101), kind=kLoop, calls=%fused_computation.3 | loop fusion | flops 14155392 | bytes 9492480 | tf_op jit(solution)/shard_map/reduce_sum | solution.py:57
  153.6 0.0 all-gather.5.cloned.1.call-done
  153.6 7.1 %fusion.16 = bf16[384,128]{1,0:T(8,128)(2,1)} fusion(bf16[6144,128]{1,0:T(8,128)(2,1)} %all-gather.5.cloned.1.call-done, f32[384,6144]{1,0:T(8,128)} %get-tuple-element.100, f32[384]{0:T(512)S(1)} %broadcast_maximum_fusion, s32[6144]{0:T(1024)S(1)} %fusion.37, s32[6144]{0:T(1024)S(1)} %add_select_fusion, s32[384]{0:T(512)S(1)} %get-tuple-element.102, ...), kind=kOutput, calls=%fused_computation.18 | convolution fusion | flops 618283008 | bytes 11165184 | tf_op jit(solution)/shard_map/dot_general | solution.py:58
  (56 shorter events, 0.2 us)
Async XLA Ops:
  6.5 129.0 %copy-start = (bf16[8192,128]{1,0:T(8,128)(2,1)S(1)}, bf16[8192,128]{1,0:T(8,128)(2,1)}, u32[]{:S(2)}) copy-start(bf16[8192,128]{1,0:T(8,128)(2,1)} %param.13) | copy-start | bytes 6291460
  6.5 129.0 %all-gather.3.cloned.1.call-start = ((), (), s32[]{:S(2)}) async-start(), calls=%async_computation.2 | async-start | bytes 1671168 | tf_op jit(solution)/shard_map/all_gather | solution.py:40
  12.5 30.4 %copy-start.3 = (s32[4]{0:T(128)S(1)}, s32[4]{0:T(128)}, u32[]{:S(2)}) copy-start(s32[4]{0:T(128)} %param.19) | copy-start | bytes 52
  12.5 44.3 %copy-start.2 = (bf16[48,96]{1,0:T(8,128)(2,1)S(1)}, bf16[48,96]{1,0:T(8,128)(2,1)}, u32[]{:S(2)}) copy-start(bf16[48,96]{1,0:T(8,128)(2,1)} %param.16) | copy-start | bytes 27652
  12.5 81.4 %copy-start.4 = (pred[6144]{0:T(1024)(128)(4,1)S(1)}, pred[6144]{0:T(1024)(128)(4,1)}, u32[]{:S(2)}) copy-start(pred[6144]{0:T(1024)(128)(4,1)} %constant.344) | copy-start | bytes 18436
  12.6 81.4 %copy-start.5 = (pred[6144]{0:T(1024)(128)(4,1)S(1)}, pred[6144]{0:T(1024)(128)(4,1)}, u32[]{:S(2)}) copy-start(pred[6144]{0:T(1024)(128)(4,1)} %constant.345) | copy-start | bytes 18436
  12.6 81.4 %copy-start.6 = (pred[6144]{0:T(1024)(128)(4,1)S(1)}, pred[6144]{0:T(1024)(128)(4,1)}, u32[]{:S(2)}) copy-start(pred[6144]{0:T(1024)(128)(4,1)} %constant.346) | copy-start | bytes 18436
  12.6 81.4 %copy-start.7 = (pred[6144]{0:T(1024)(128)(4,1)S(1)}, pred[6144]{0:T(1024)(128)(4,1)}, u32[]{:S(2)}) copy-start(pred[6144]{0:T(1024)(128)(4,1)} %constant.347) | copy-start | bytes 18436
  12.6 81.4 %copy-start.8 = (pred[6144]{0:T(1024)(128)(4,1)S(1)}, pred[6144]{0:T(1024)(128)(4,1)}, u32[]{:S(2)}) copy-start(pred[6144]{0:T(1024)(128)(4,1)} %constant.348) | copy-start | bytes 18436
  12.6 81.4 %copy-start.9 = (pred[6144]{0:T(1024)(128)(4,1)S(1)}, pred[6144]{0:T(1024)(128)(4,1)}, u32[]{:S(2)}) copy-start(pred[6144]{0:T(1024)(128)(4,1)} %constant.349) | copy-start | bytes 18436
  12.6 81.4 %copy-start.10 = (pred[6144]{0:T(1024)(128)(4,1)S(1)}, pred[6144]{0:T(1024)(128)(4,1)}, u32[]{:S(2)}) copy-start(pred[6144]{0:T(1024)(128)(4,1)} %constant.350) | copy-start | bytes 18436
  12.6 81.4 %copy-start.11 = (pred[6144]{0:T(1024)(128)(4,1)S(1)}, pred[6144]{0:T(1024)(128)(4,1)}, u32[]{:S(2)}) copy-start(pred[6144]{0:T(1024)(128)(4,1)} %constant.351) | copy-start | bytes 18436
  12.6 81.4 %copy-start.12 = (pred[6144]{0:T(1024)(128)(4,1)S(1)}, pred[6144]{0:T(1024)(128)(4,1)}, u32[]{:S(2)}) copy-start(pred[6144]{0:T(1024)(128)(4,1)} %constant.352) | copy-start | bytes 18436
  12.7 81.4 %copy-start.13 = (pred[6144]{0:T(1024)(128)(4,1)S(1)}, pred[6144]{0:T(1024)(128)(4,1)}, u32[]{:S(2)}) copy-start(pred[6144]{0:T(1024)(128)(4,1)} %constant.353) | copy-start | bytes 18436
  12.7 81.4 %copy-start.14 = (pred[6144]{0:T(1024)(128)(4,1)S(1)}, pred[6144]{0:T(1024)(128)(4,1)}, u32[]{:S(2)}) copy-start(pred[6144]{0:T(1024)(128)(4,1)} %constant.354) | copy-start | bytes 18436
  12.7 81.4 %copy-start.15 = (pred[6144]{0:T(1024)(128)(4,1)S(1)}, pred[6144]{0:T(1024)(128)(4,1)}, u32[]{:S(2)}) copy-start(pred[6144]{0:T(1024)(128)(4,1)} %constant.355) | copy-start | bytes 18436
  12.7 81.4 %copy-start.16 = (pred[6144]{0:T(1024)(128)(4,1)S(1)}, pred[6144]{0:T(1024)(128)(4,1)}, u32[]{:S(2)}) copy-start(pred[6144]{0:T(1024)(128)(4,1)} %constant.356) | copy-start | bytes 18436
  12.7 81.4 %copy-start.17 = (pred[6144]{0:T(1024)(128)(4,1)S(1)}, pred[6144]{0:T(1024)(128)(4,1)}, u32[]{:S(2)}) copy-start(pred[6144]{0:T(1024)(128)(4,1)} %constant.357) | copy-start | bytes 18436
  12.7 81.4 %copy-start.18 = (pred[6144]{0:T(1024)(128)(4,1)S(1)}, pred[6144]{0:T(1024)(128)(4,1)}, u32[]{:S(2)}) copy-start(pred[6144]{0:T(1024)(128)(4,1)} %constant.358) | copy-start | bytes 18436
  12.7 81.4 %copy-start.19 = (pred[6144]{0:T(1024)(128)(4,1)S(1)}, pred[6144]{0:T(1024)(128)(4,1)}, u32[]{:S(2)}) copy-start(pred[6144]{0:T(1024)(128)(4,1)} %constant.359) | copy-start | bytes 18436
  12.7 81.4 %copy-start.20 = (pred[6144]{0:T(1024)(128)(4,1)S(1)}, pred[6144]{0:T(1024)(128)(4,1)}, u32[]{:S(2)}) copy-start(pred[6144]{0:T(1024)(128)(4,1)} %constant.360) | copy-start | bytes 18436
  12.8 81.4 %copy-start.21 = (pred[6144]{0:T(1024)(128)(4,1)S(1)}, pred[6144]{0:T(1024)(128)(4,1)}, u32[]{:S(2)}) copy-start(pred[6144]{0:T(1024)(128)(4,1)} %constant.361) | copy-start | bytes 18436
  12.8 81.4 %copy-start.22 = (pred[6144]{0:T(1024)(128)(4,1)S(1)}, pred[6144]{0:T(1024)(128)(4,1)}, u32[]{:S(2)}) copy-start(pred[6144]{0:T(1024)(128)(4,1)} %constant.362) | copy-start | bytes 18436
  12.8 81.4 %copy-start.23 = (pred[6144]{0:T(1024)(128)(4,1)S(1)}, pred[6144]{0:T(1024)(128)(4,1)}, u32[]{:S(2)}) copy-start(pred[6144]{0:T(1024)(128)(4,1)} %constant.363) | copy-start | bytes 18436
  12.8 81.4 %copy-start.24 = (pred[6144]{0:T(1024)(128)(4,1)S(1)}, pred[6144]{0:T(1024)(128)(4,1)}, u32[]{:S(2)}) copy-start(pred[6144]{0:T(1024)(128)(4,1)} %constant.364) | copy-start | bytes 18436
  12.8 81.4 %copy-start.25 = (pred[6144]{0:T(1024)(128)(4,1)S(1)}, pred[6144]{0:T(1024)(128)(4,1)}, u32[]{:S(2)}) copy-start(pred[6144]{0:T(1024)(128)(4,1)} %constant.365) | copy-start | bytes 18436
  12.8 81.4 %copy-start.26 = (pred[6144]{0:T(1024)(128)(4,1)S(1)}, pred[6144]{0:T(1024)(128)(4,1)}, u32[]{:S(2)}) copy-start(pred[6144]{0:T(1024)(128)(4,1)} %constant.366) | copy-start | bytes 18436
  12.8 81.4 %copy-start.27 = (pred[6144]{0:T(1024)(128)(4,1)S(1)}, pred[6144]{0:T(1024)(128)(4,1)}, u32[]{:S(2)}) copy-start(pred[6144]{0:T(1024)(128)(4,1)} %constant.367) | copy-start | bytes 18436
  12.8 81.4 %copy-start.28 = (pred[6144]{0:T(1024)(128)(4,1)S(1)}, pred[6144]{0:T(1024)(128)(4,1)}, u32[]{:S(2)}) copy-start(pred[6144]{0:T(1024)(128)(4,1)} %constant.368) | copy-start | bytes 18436
  12.9 81.4 %copy-start.29 = (pred[6144]{0:T(1024)(128)(4,1)S(1)}, pred[6144]{0:T(1024)(128)(4,1)}, u32[]{:S(2)}) copy-start(pred[6144]{0:T(1024)(128)(4,1)} %constant.369) | copy-start | bytes 18436
  12.9 81.4 %copy-start.30 = (pred[6144]{0:T(1024)(128)(4,1)S(1)}, pred[6144]{0:T(1024)(128)(4,1)}, u32[]{:S(2)}) copy-start(pred[6144]{0:T(1024)(128)(4,1)} %constant.370) | copy-start | bytes 18436
  12.9 81.4 %copy-start.31 = (pred[6144]{0:T(1024)(128)(4,1)S(1)}, pred[6144]{0:T(1024)(128)(4,1)}, u32[]{:S(2)}) copy-start(pred[6144]{0:T(1024)(128)(4,1)} %constant.371) | copy-start | bytes 18436
  12.9 81.4 %copy-start.32 = (pred[6144]{0:T(1024)(128)(4,1)S(1)}, pred[6144]{0:T(1024)(128)(4,1)}, u32[]{:S(2)}) copy-start(pred[6144]{0:T(1024)(128)(4,1)} %constant.372) | copy-start | bytes 18436
  12.9 81.4 %copy-start.33 = (pred[6144]{0:T(1024)(128)(4,1)S(1)}, pred[6144]{0:T(1024)(128)(4,1)}, u32[]{:S(2)}) copy-start(pred[6144]{0:T(1024)(128)(4,1)} %constant.373) | copy-start | bytes 18436
  12.9 81.4 %copy-start.34 = (pred[6144]{0:T(1024)(128)(4,1)S(1)}, pred[6144]{0:T(1024)(128)(4,1)}, u32[]{:S(2)}) copy-start(pred[6144]{0:T(1024)(128)(4,1)} %constant.374) | copy-start | bytes 18436
  12.9 81.4 %copy-start.35 = (pred[6144]{0:T(1024)(128)(4,1)S(1)}, pred[6144]{0:T(1024)(128)(4,1)}, u32[]{:S(2)}) copy-start(pred[6144]{0:T(1024)(128)(4,1)} %constant.375) | copy-start | bytes 18436
  12.9 81.3 %copy-start.36 = (pred[6144]{0:T(1024)(128)(4,1)S(1)}, pred[6144]{0:T(1024)(128)(4,1)}, u32[]{:S(2)}) copy-start(pred[6144]{0:T(1024)(128)(4,1)} %constant.376) | copy-start | bytes 18436
  13.0 81.3 %copy-start.37 = (pred[6144]{0:T(1024)(128)(4,1)S(1)}, pred[6144]{0:T(1024)(128)(4,1)}, u32[]{:S(2)}) copy-start(pred[6144]{0:T(1024)(128)(4,1)} %constant.377) | copy-start | bytes 18436
  13.0 81.3 %copy-start.38 = (pred[6144]{0:T(1024)(128)(4,1)S(1)}, pred[6144]{0:T(1024)(128)(4,1)}, u32[]{:S(2)}) copy-start(pred[6144]{0:T(1024)(128)(4,1)} %constant.378) | copy-start | bytes 18436
  13.0 81.3 %copy-start.39 = (pred[6144]{0:T(1024)(128)(4,1)S(1)}, pred[6144]{0:T(1024)(128)(4,1)}, u32[]{:S(2)}) copy-start(pred[6144]{0:T(1024)(128)(4,1)} %constant.379) | copy-start | bytes 18436
  13.0 81.3 %copy-start.40 = (pred[6144]{0:T(1024)(128)(4,1)S(1)}, pred[6144]{0:T(1024)(128)(4,1)}, u32[]{:S(2)}) copy-start(pred[6144]{0:T(1024)(128)(4,1)} %constant.380) | copy-start | bytes 18436
  20.9 35.8 %all-to-all-start = ((bf16[48,2,512]{2,1,0:T(2,128)(2,1)}), bf16[48,2,512]{2,1,0:T(2,128)(2,1)S(1)}, u32[]{:S(2)}, u32[]{:S(2)}) async-start(bf16[48,2,512]{2,1,0:T(2,128)(2,1)} %reshape.368), calls=%async_computation | async-start | bytes 196608 | tf_op jit(solution)/shard_map/all_to_all | solution.py:30
  58.8 29.2 %all-to-all-start.1 = ((bf16[48,8,128]{2,1,0:T(8,128)(2,1)}), bf16[48,8,128]{2,1,0:T(8,128)(2,1)S(1)}, u32[]{:S(2)}, u32[]{:S(2)}) async-start(bf16[48,8,128]{2,1,0:T(8,128)(2,1)} %copy.20), calls=%async_computation.1 | async-start | bytes 196608 | tf_op jit(solution)/shard_map/all_to_all | solution.py:35
  72.4 81.2 %all-gather.5.cloned.1.call-start = ((), (), s32[]{:S(2)}) async-start(), calls=%async_computation.3 | async-start | bytes 1671168 | tf_op jit(solution)/shard_map/all_gather | solution.py:41
  88.0 0.6 copy-start.1
Sparse Core Ops, SparseCore 0:
  12.7 47.6 all-gather.2
  88.8 28.2 all-gather.4
where the time goes:
time: 169 us; the launch traced here: 168 us
  other arithmetic  51.3 us (30%)
  starting transfers between devices  34 us (20%)
  matrix products  32.1 us (19%)
  waiting for transfers between devices  15.3 us (9%)
  between operations  14.7 us (9%)
  blocking collectives  12.2 us (7%)
  local copies, waits for them, and re-layouts  8.02 us (5%)
    add x1, other arithmetic, shards(): jnp.repeat(block_all, BLK, total_repeat_length=count) * BLK + offsets % BLK  41.1 us
    all_to_all x1, starting transfers between devices, shards(): lax.all_to_all(value_rows[None], 'tensor', split_axis=1, concat_axis=0, t...  20.2 us
    all_to_all x1, waiting for transfers between devices, shards(): lax.all_to_all(mixed_here, 'tensor', split_axis=0, concat_axis=1, tiled=T...  13.9 us
    all_to_all x1, starting transfers between devices, shards(): lax.all_to_all(mixed_here, 'tensor', split_axis=0, concat_axis=1, tiled=T...  13.6 us
    dot_general x1, matrix products, shards(): lax.dot_general(query_rows, key_piece, (((1,), (1,)), ((), ())), preferre...  12.3 us
    unnamed x1, blocking collectives  12.2 us
    dot_general x1, matrix products, shards(): jnp.dot(weights.astype(jnp.bfloat16), value_piece, preferred_element_type...  7.08 us
    dot_general x1, matrix products, shards(): jnp.dot(tokens, w_key, preferred_element_type=jnp.float32)  5.98 us
  transfers between devices with their start and end apart: 4, of which 2 were waited for; matrix products, arithmetic and copies ran while one was open for 46% of the time, Pallas kernels for 0%

commit v1 on v0

v1 whole, which is shorter than its diff:
```python
import jax
import jax.numpy as jnp
from jax import lax
from jax.experimental import pallas as pl
from jax.experimental.pallas import tpu as pltpu
from jax.sharding import PartitionSpec as P


HEAD_DIM = 128
BLK = 96
PAD = 16
CORE_GROUPS = [[2 * k + core for k in range(8)] for core in range(2)]
VMEM = pltpu.MemorySpace.VMEM
SMEM = pltpu.MemorySpace.SMEM


def on_chip(x):
    return pltpu.with_memory_space_constraint(x, VMEM)


def value_kernel(x_ref, w_ref, out_ref, acc_ref):
    step = pl.program_id(0)
    part = jnp.dot(x_ref[...], w_ref[...], preferred_element_type=jnp.float32)

    @pl.when(step == 0)
    def _():
        acc_ref[...] = part

    @pl.when(step > 0)
    def _():
        acc_ref[...] += part

    @pl.when(step == pl.num_programs(0) - 1)
    def _():
        out_ref[...] = acc_ref[...].astype(out_ref.dtype)


def project_values(tokens, w_value, depth=2048):
    rows, width = tokens.shape
    cols = w_value.shape[1]
    return pl.pallas_call(
        value_kernel,
        grid=(width // depth,),
        in_specs=[
            pl.BlockSpec((rows, depth), lambda k: (0, k)),
            pl.BlockSpec((depth, cols), lambda k: (k, 0)),
        ],
        out_specs=pl.BlockSpec((rows, cols), lambda k: (0, 0)),
        out_shape=jax.ShapeDtypeStruct((rows, cols), jnp.bfloat16),
        scratch_shapes=[pltpu.VMEM((rows, cols), jnp.float32)],
        name="project_values",
    )(tokens, w_value)


def query_key_kernel(ids_ref, x_ref, wq_ref, wk_ref, q_ref, k_ref, acc_ref):
    step = pl.program_id(0)
    rows = x_ref.shape[0]
    cols = wq_ref.shape[1]
    both = jnp.concatenate([wq_ref[...], wk_ref[...]], axis=1)
    part = jnp.dot(x_ref[...], both, preferred_element_type=jnp.float32)

    @pl.when(step == 0)
    def _():
        acc_ref[...] = part

    @pl.when(step > 0)
    def _():
        acc_ref[...] += part

    @pl.when(step == pl.num_programs(0) - 1)
    def _():
        q_ref[...] = acc_ref[:, :cols].astype(q_ref.dtype)
        keys = acc_ref[:, cols:].astype(k_ref.dtype)
        row = lax.broadcasted_iota(jnp.int32, (PAD, cols), 0)
        ids = jnp.zeros((PAD, cols), jnp.float32)
        for j in range(4):
            ids = jnp.where(row == j, ids_ref[j].astype(jnp.float32), ids)
        k_ref[0, :rows, :] = keys
        k_ref[0, rows:, :] = ids.astype(k_ref.dtype)


def project_queries_keys(block_ids, tokens, w_query, w_key, depth=2048):
    rows, width = tokens.shape
    cols = w_query.shape[1]
    return pl.pallas_call(
        query_key_kernel,
        grid=(width // depth,),
        in_specs=[
            pl.BlockSpec(memory_space=SMEM),
            pl.BlockSpec((rows, depth), lambda k: (0, k)),
            pl.BlockSpec((depth, cols), lambda k: (k, 0)),
            pl.BlockSpec((depth, cols), lambda k: (k, 0)),
        ],
        out_specs=[
            pl.BlockSpec((rows, cols), lambda k: (0, 0)),
            pl.BlockSpec((1, rows + PAD, cols), lambda k: (0, 0, 0)),
        ],
        out_shape=[
            jax.ShapeDtypeStruct((rows, cols), jnp.bfloat16),
            jax.ShapeDtypeStruct((1, rows + PAD, cols), jnp.bfloat16),
        ],
        scratch_shapes=[pltpu.VMEM((rows, 2 * cols), jnp.float32)],
        name="project_queries_keys",
    )(block_ids, tokens, w_query, w_key)


def mix_kernel(u_ref, w_in_ref, w_out_ref, out_ref, wide_ref):
    count = u_ref.shape[1]
    hidden_units = w_in_ref.shape[0] // 2
    wide_ref[...] = u_ref[...].astype(jnp.float32)
    flat = jnp.concatenate([wide_ref[:, t, :] for t in range(count)], axis=1)
    parts = jnp.dot(w_in_ref[...], flat.astype(jnp.bfloat16), preferred_element_type=jnp.float32)
    hidden = (jax.nn.silu(parts[:hidden_units]) * parts[hidden_units:]).astype(jnp.bfloat16)
    mixed = flat + jnp.dot(w_out_ref[...], hidden, preferred_element_type=jnp.float32)
    for t in range(count):
        wide_ref[:, t, :] = mixed[:, t * HEAD_DIM : (t + 1) * HEAD_DIM]
    out_ref[...] = wide_ref[...].astype(out_ref.dtype)


def mix(gathered, w_in, w_out):
    return pl.pallas_call(
        mix_kernel,
        in_specs=[pl.BlockSpec(memory_space=VMEM)] * 3,
        out_specs=pl.BlockSpec(memory_space=VMEM),
        out_shape=jax.ShapeDtypeStruct(gathered.shape, jnp.bfloat16),
        scratch_shapes=[pltpu.VMEM(gathered.shape, jnp.float32)],
        name="mix_heads",
    )(on_chip(gathered), w_in, w_out)


def weight_kernel(ids_ref, q_ref, k0_ref, k1_ref, k2_ref, k3_ref, w_ref, total_ref, s_ref):
    half = q_ref.shape[0] // 2
    rows = q_ref.shape[0]
    chunk = 2 * half
    scale = HEAD_DIM ** (-0.5)
    q_row = lax.broadcasted_iota(jnp.int32, (half, 1), 0)
    lane = lax.broadcasted_iota(jnp.int32, (1, chunk), 1)
    lane_off = lane % BLK
    lane_blk = lane // BLK
    for s in range(2):
        id_lo, id_hi = ids_ref[2 * s], ids_ref[2 * s + 1]
        q_pos = jnp.where(q_row < BLK, id_lo * BLK + q_row, id_hi * BLK + q_row - BLK)
        queries = q_ref[s * half : (s + 1) * half, :]
        top = jnp.full((half, chunk), -1e30, jnp.float32)
        at = 0
        for k_ref in (k0_ref, k1_ref, k2_ref, k3_ref):
            for d in range(0, k_ref.shape[0], 2):
                keys = jnp.concatenate(
                    [k_ref[d + e, s * half : (s + 1) * half, :] for e in range(2)], axis=0
                )
                k_ids = jnp.zeros((1, chunk), jnp.float32)
                for e in range(2):
                    tail = k_ref[d + e, rows:, :].astype(jnp.float32)
                    for j in range(2):
                        wide = jnp.concatenate([tail[2 * s + j : 2 * s + j + 1, :]] * 3, axis=1)
                        k_ids = jnp.where(lane_blk == 2 * e + j, wide, k_ids)
                k_pos = k_ids.astype(jnp.int32) * BLK + lane_off
                scores = (
                    lax.dot_general(
                        queries, keys, (((1,), (1,)), ((), ())), preferred_element_type=jnp.float32
                    )
                    * scale
                )
                scores = jnp.where(k_pos <= q_pos, scores, -1e30)
                s_ref[:, at : at + chunk] = scores
                top = jnp.maximum(top, scores)
                at += chunk
        top = jnp.max(top, axis=1, keepdims=True)
        total = jnp.zeros((half, chunk), jnp.float32)
        for at in range(0, s_ref.shape[1], chunk):
            weights = jnp.exp(s_ref[:, at : at + chunk] - top)
            total = total + weights
            w_ref[s, :, at : at + chunk] = weights.astype(w_ref.dtype)
        total = jnp.sum(total, axis=1, keepdims=True)
        total_ref[s * half : (s + 1) * half, :] = jnp.broadcast_to(total, (half, HEAD_DIM))


def attention_weights(block_ids, queries, keys):
    rows = queries.shape[0]
    half = rows // 2
    count = sum(piece.shape[0] for piece in keys) * half
    return pl.pallas_call(
        weight_kernel,
        in_specs=[pl.BlockSpec(memory_space=SMEM)] + [pl.BlockSpec(memory_space=VMEM)] * 5,
        out_specs=[pl.BlockSpec(memory_space=VMEM)] * 2,
        out_shape=[
            jax.ShapeDtypeStruct((2, half, count), jnp.bfloat16),
            jax.ShapeDtypeStruct((rows, HEAD_DIM), jnp.float32),
        ],
        scratch_shapes=[pltpu.VMEM((half, count), jnp.float32)],
        name="attention_weights",
    )(block_ids, queries, *[on_chip(piece) for piece in keys])


def apply_kernel(spot_ref, w_ref, total_ref, v0_ref, v1_ref, out_ref):
    half = out_ref.shape[0] // 2
    sources = 4
    for s in range(2):
        acc = jnp.zeros((half, HEAD_DIM), jnp.float32)
        at = 0
        for v_ref in (v0_ref, v1_ref):
            for d in range(0, v_ref.shape[0], sources):
                values = jnp.concatenate(
                    [v_ref[spot_ref[d + e], s * half : (s + 1) * half, :] for e in range(sources)],
                    axis=0,
                )
                acc = acc + jnp.dot(
                    w_ref[s, :, at : at + sources * half],
                    values,
                    preferred_element_type=jnp.float32,
                )
                at += sources * half
        total = total_ref[s * half : (s + 1) * half, :]
        out_ref[s * half : (s + 1) * half, :] = (acc / total).astype(out_ref.dtype)


def apply_weights(spots, weights, total, values_mine, values_other):
    return pl.pallas_call(
        apply_kernel,
        in_specs=[pl.BlockSpec(memory_space=SMEM)] + [pl.BlockSpec(memory_space=VMEM)] * 4,
        out_specs=pl.BlockSpec(memory_space=VMEM),
        out_shape=jax.ShapeDtypeStruct(total.shape, jnp.bfloat16),
        name="apply_weights",
    )(spots, weights, total, on_chip(values_mine), on_chip(values_other))


def shards(tokens, w_query, w_key, w_value, mix_gate, mix_up, mix_down, block_ids):
    heads = mix_gate.shape[0]
    rows = tokens.shape[0]

    def exchange(x):
        return lax.all_to_all(x, "tensor", split_axis=0, concat_axis=0, tiled=True)

    def spread(x):
        return lax.all_to_all(
            x, "context", split_axis=0, concat_axis=0, axis_index_groups=CORE_GROUPS, tiled=True
        )

    def flip(x, bit):
        return lax.ppermute(x, "context", [(i, i ^ bit) for i in range(16)])

    def doubled(x, bit):
        return jnp.concatenate([x, flip(x, bit)], axis=0)

    w_in = jnp.concatenate([mix_gate, mix_up], axis=1).T
    w_out = mix_down.T
    values = project_values(tokens, w_value)
    gathered = exchange(values.reshape(heads, rows // heads, HEAD_DIM))
    tokens, values = lax.optimization_barrier((tokens, values))
    queries, keys = project_queries_keys(block_ids, tokens, w_query, w_key)
    keys = doubled(keys, 2)
    keys = doubled(keys, 8)
    near = flip(keys, 4)
    keys = [keys, near, flip(keys, 1), flip(near, 1)]
    turn = jnp.arange(8, dtype=jnp.int32)
    spots = (lax.axis_index("context") // 2) ^ (turn % 2 + turn // 2 % 2 * 4 + turn // 4 * 2)
    mixed = mix(gathered, w_in, w_out)
    mixed_rows = exchange(mixed).reshape(1, rows, HEAD_DIM)
    weights, total = attention_weights(block_ids, queries, keys)
    values_mine = spread(jnp.broadcast_to(mixed_rows, (8, rows, HEAD_DIM)))
    values_other = flip(values_mine, 1)
    return apply_weights(spots, weights, total, values_mine, values_other)


def solution(mesh):
    in_specs = (
        P("context", None),
        P(None, "tensor"),
        P(None, "tensor"),
        P(None, "tensor"),
        P(),
        P(),
        P(),
        P("context"),
    )
    out_specs = P("context", "tensor")
    return jax.shard_map(shards, mesh=mesh, in_specs=in_specs, out_specs=out_specs, check_vma=False)
```

time: 169 us -> 117 us (0.69)
  the two profiles are of different devices: /device:TPU:8 before, /device:TPU:13 now
where the time goes in v1:
time: 117 us; the launch traced here: 116 us
  starting transfers between devices  49.2 us (42%)
  waiting for transfers between devices  22.2 us (19%)
  Pallas kernels  21.3 us (18%)
  blocking collectives  18.9 us (16%)
  local copies, waits for them, and re-layouts  2.16 us (2%)
  other arithmetic  2.16 us (2%)
    ppermute x6, starting transfers between devices, flip(): return lax.ppermute(x, 'context', [(i, i ^ bit) for i in range(16)])  24.2 us
    all_to_all x1, starting transfers between devices, exchange(): return lax.all_to_all(x, 'tensor', split_axis=0, concat_axis=0, tiled=True)  19.9 us
    all_to_all x1, blocking collectives, exchange(): return lax.all_to_all(x, 'tensor', split_axis=0, concat_axis=0, tiled=True)  18.9 us
    all_to_all x1, waiting for transfers between devices, exchange(): return lax.all_to_all(x, 'tensor', split_axis=0, concat_axis=0, tiled=True)  13.4 us
    ppermute x6, waiting for transfers between devices, flip(): return lax.ppermute(x, 'context', [(i, i ^ bit) for i in range(16)])  8.75 us
    pallas_call x1, Pallas kernels, project_queries_keys(): pl.pallas_call(query_key_kernel, grid=(width // depth,), in_specs=[pl.Blo...  6.28 us
    pallas_call x1, Pallas kernels, project_values(): pl.pallas_call(value_kernel, grid=(width // depth,), in_specs=[pl.BlockSp...  5.69 us
    all_to_all x1, starting transfers between devices, spread(): lax.all_to_all(x, 'context', split_axis=0, concat_axis=0, axis_index_grou...  5.14 us
  transfers between devices with their start and end apart: 8, of which 4 were waited for; matrix products, arithmetic and copies ran while one was open for 3% of the time, Pallas kernels for 9%

profile of v1, /device:TPU:13, one launch (start us, length us, event | category | flops | bytes accessed | tf_op | source)
XLA Modules:
  0.0 116.0 jit_solution(15817909343845896223)
XLA Ops:
  0.0 0.0 copy-start
  0.0 0.0 copy-start.1
  0.0 5.7 %project_values.1 = bf16[384,128]{1,0:T(8,128)(2,1)} custom-call(bf16[384,8192]{1,0:T(8,128)(2,1)} %x_ref.2, bf16[8192,128]{1,0:T(8,128)(2,1)} %w_ref.1), custom_call_target="tpu_custom_call" | custom-call | tf_op jit(solution)/shard_map/project_values/pallas_call | solution.py:41
  5.7 19.9 %all-to-all-start = ((bf16[48,8,128]{2,1,0:T(8,128)(2,1)}), bf16[48,8,128]{2,1,0:T(8,128)(2,1)S(1)}, u32[]{:S(2)}, u32[]{:S(2)}) async-start(bf16[48,8,128]{2,1,0:T(8,128)(2,1)} %bitcast.5), calls=%async_computation | async-start | bytes 196608 | tf_op jit(solution)/shard_map/all_to_all | solution.py:232
  25.6 0.0 copy-done
  25.6 0.1 copy.10
  25.7 0.0 copy-done.1
  25.7 0.1 copy.9
  25.8 0.6 maximum_bitcast_fusion.w_in_ref
  26.5 13.4 %all-to-all-done.u_ref = bf16[48,8,128]{2,1,0:T(8,128)(2,1)S(1)} async-done(((bf16[48,8,128]{2,1,0:T(8,128)(2,1)}), bf16[48,8,128]{2,1,0:T(8,128)(2,1)S(1)}, u32[]{:S(2)}, u32[]{:S(2)}) %all-to-all-start) | async-done | bytes 98336 | tf_op jit(solution)/shard_map/all_to_all | solution.py:232
  39.9 1.9 %mix_heads.1 = bf16[48,8,128]{2,1,0:T(8,128)(2,1)} custom-call(bf16[48,8,128]{2,1,0:T(8,128)(2,1)S(1)} %all-to-all-done.u_ref, bf16[192,48]{1,0:T(8,128)(2,1)} %maximum_bitcast_fusion.w_in_ref, bf16[48,96]{1,0:T(8,128)(2,1)} %bitcast.7), custom_call_target="tpu_custom_call" | custom-call | tf_op jit(solution)/shard_map/mix_heads/pallas_call | solution.py:121
  41.8 18.9 %all_to_all.15 = bf16[48,8,128]{2,1,0:T(8,128)(2,1)S(1)} all-to-all(bf16[48,8,128]{2,1,0:T(8,128)(2,1)} %mix_heads.1), channel_id=1, replica_groups=mesh['tensor'=48,'context'=16] {'tensor'}, dimensions={0} | all-to-all | bytes 196608 | tf_op jit(solution)/shard_map/all_to_all | solution.py:232
  60.8 1.0 broadcast_in_dim.8
  61.8 5.1 %all-to-all-start.2 = ((bf16[8,384,128]{2,1,0:T(8,128)(2,1)}), bf16[8,384,128]{2,1,0:T(8,128)(2,1)S(1)}, u32[]{:S(2)}, u32[]{:S(2)}) async-start(bf16[8,384,128]{2,1,0:T(8,128)(2,1)} %broadcast_in_dim.8), calls=%async_computation.2 | async-start | bytes 1572864 | tf_op jit(solution)/shard_map/all_to_all | solution.py:235
  66.9 6.3 %project_queries_keys.1 = (bf16[384,128]{1,0:T(8,128)(2,1)}, bf16[1,400,128]{2,1,0:T(8,128)(2,1)}) custom-call(s32[4]{0:T(128)} %ids_ref.3, bf16[384,8192]{1,0:T(8,128)(2,1)} %x_ref.2, bf16[8192,128]{1,0:T(8,128)(2,1)} %wq_ref.1, bf16[8192,128]{1,0:T(8,128)(2,1)} %wk_ref.1), custom_call_target="tpu_custom_call" | custom-call | tf_op jit(solution)/shard_map/project_queries_keys/pallas_call | solution.py:85
  73.2 2.2 %collective-permute-start = (bf16[1,400,128]{2,1,0:T(8,128)(2,1)}, bf16[1,400,128]{2,1,0:T(8,128)(2,1)S(1)}, u32[]{:S(2)}, u32[]{:S(2)}) collective-permute-start(bf16[1,400,128]{2,1,0:T(8,128)(2,1)} %get-tuple-element.12), channel_id=1, source_target_pairs={{0,2},{1,3},{2,0},{3,1},{4,6},{5,7},{6,4},{7,5},{8,10},{9,11},{10,... | collective-permute-start | bytes 307208 | tf_op jit(solution)/shard_map/ppermute | solution.py:240
  75.4 3.4 %collective-permute-done = bf16[1,400,128]{2,1,0:T(8,128)(2,1)S(1)} collective-permute-done((bf16[1,400,128]{2,1,0:T(8,128)(2,1)}, bf16[1,400,128]{2,1,0:T(8,128)(2,1)S(1)}, u32[]{:S(2)}, u32[]{:S(2)}) %collective-permute-start) | collective-permute-done | bytes 102432 | tf_op jit(solution)/shard_map/ppermute | solution.py:240
  78.8 0.9 pad_maximum_fusion
  79.7 2.5 %collective-permute-start.1 = (bf16[2,400,128]{2,1,0:T(8,128)(2,1)S(1)}, bf16[2,400,128]{2,1,0:T(8,128)(2,1)S(1)}, u32[]{:S(2)}, u32[]{:S(2)}) collective-permute-start(bf16[2,400,128]{2,1,0:T(8,128)(2,1)S(1)} %pad_maximum_fusion), channel_id=1, source_target_pairs={{0,8},{1,9},{2,10},{3,11},{4,12},{5,13},{6,14},{7,15},{8,0},{9,1},... | collective-permute-start | bytes 614408 | tf_op jit(solution)/shard_map/ppermute | solution.py:240
  82.2 0.9 constant_dynamic-update-slice_fusion.2
  83.1 4.6 %collective-permute-done.1 = bf16[2,400,128]{2,1,0:T(8,128)(2,1)S(1)} collective-permute-done((bf16[2,400,128]{2,1,0:T(8,128)(2,1)S(1)}, bf16[2,400,128]{2,1,0:T(8,128)(2,1)S(1)}, u32[]{:S(2)}, u32[]{:S(2)}) %collective-permute-start.1) | collective-permute-done | bytes 204832 | tf_op jit(solution)/shard_map/ppermute | solution.py:240
  87.7 2.8 %collective-permute-start.2 = (bf16[4,400,128]{2,1,0:T(8,128)(2,1)S(1)}, bf16[4,400,128]{2,1,0:T(8,128)(2,1)S(1)}, u32[]{:S(2)}, u32[]{:S(2)}) collective-permute-start(bf16[4,400,128]{2,1,0:T(8,128)(2,1)S(1)} %constant_dynamic-update-slice_fusion.k0_ref), channel_id=1, source_target_pairs={{0,4},{1,5},{2,6},{3,7},{4,0},{5,1},{6,2},{7,3},{8,12},{9,13},{10,... | collective-permute-start | bytes 1228808 | tf_op jit(solution)/shard_map/ppermute | solution.py:240
  90.5 0.0 all-to-all-done.2.v0_ref
  90.6 9.7 %collective-permute-start.5 = (bf16[8,384,128]{2,1,0:T(8,128)(2,1)S(1)}, bf16[8,384,128]{2,1,0:T(8,128)(2,1)S(1)}, u32[]{:S(2)}, u32[]{:S(2)}) collective-permute-start(bf16[8,384,128]{2,1,0:T(8,128)(2,1)S(1)} %all-to-all-done.2.v0_ref), channel_id=1, source_target_pairs={{0,1},{1,0},{2,3},{3,2},{4,5},{5,4},{6,7},{7,6},{8,9},{9,8},{10,11... | collective-permute-start | bytes 2359304 | tf_op jit(solution)/shard_map/ppermute | solution.py:240
  100.3 1.9 %collective-permute-start.3 = (bf16[4,400,128]{2,1,0:T(8,128)(2,1)S(1)}, bf16[4,400,128]{2,1,0:T(8,128)(2,1)S(1)}, u32[]{:S(2)}, u32[]{:S(2)}) collective-permute-start(bf16[4,400,128]{2,1,0:T(8,128)(2,1)S(1)} %constant_dynamic-update-slice_fusion.k0_ref), channel_id=1, source_target_pairs={{0,1},{1,0},{2,3},{3,2},{4,5},{5,4},{6,7},{7,6},{8,9},{9,8},{10,11... | collective-permute-start | bytes 1228808 | tf_op jit(solution)/shard_map/ppermute | solution.py:240
  102.2 0.0 collective-permute-done.2.k1_ref
  102.2 5.1 %collective-permute-start.4 = (bf16[4,400,128]{2,1,0:T(8,128)(2,1)S(1)}, bf16[4,400,128]{2,1,0:T(8,128)(2,1)S(1)}, u32[]{:S(2)}, u32[]{:S(2)}) collective-permute-start(bf16[4,400,128]{2,1,0:T(8,128)(2,1)S(1)} %collective-permute-done.2.k1_ref), channel_id=1, source_target_pairs={{0,1},{1,0},{2,3},{3,2},{4,5},{5,4},{6,7},{7,6},{8,9},{9,8},{10,11... | collective-permute-start | bytes 1228808 | tf_op jit(solution)/shard_map/ppermute | solution.py:240
  107.3 0.6 fusion.3.spot_ref
  107.9 0.0 collective-permute-done.3.k2_ref
  107.9 0.7 collective-permute-done.4.k3_ref
  108.6 4.3 %attention_weights.1 = (bf16[2,192,3072]{2,1,0:T(8,128)(2,1)}, f32[384,128]{1,0:T(8,128)}) custom-call(s32[4]{0:T(128)} %ids_ref.3, bf16[384,128]{1,0:T(8,128)(2,1)} %get-tuple-element.11.q_ref, bf16[4,400,128]{2,1,0:T(8,128)(2,1)S(1)} %constant_dynamic-update-slice_fusion.k0_ref, bf16[4,400,128]{2,1,0:T(8,128)(2,1)S(1)} %collective-permute-done.2.k1_ref, ...), custom_call_target="tpu_custom_call" | custom-call | tf_op jit(solution)/shard_map/attention_weights/pallas_call | solution.py:182
  112.9 0.0 collective-permute-done.5.v1_ref
  112.9 3.1 %apply_weights.1 = bf16[384,128]{1,0:T(8,128)(2,1)} custom-call(s32[8]{0:T(128)} %fusion.3.spot_ref, bf16[2,192,3072]{2,1,0:T(8,128)(2,1)} %get-tuple-element.13.w_ref, f32[384,128]{1,0:T(8,128)} %get-tuple-element.14.total_ref, bf16[8,384,128]{2,1,0:T(8,128)(2,1)S(1)} %all-to-all-done.2.v0_ref, bf16[8,384,128]{2,1,0:T(8,128)(2,1)S(1)} %collective-permute-done.5.v1_ref), custom_call_target="tpu_custom_call" | custom-call | tf_op jit(solution)/shard_map/apply_weights/pallas_call | solution.py:218
  (2 shorter events, 0.0 us)
Async XLA Ops:
  0.0 25.6 %copy-start = (bf16[48,96]{1,0:T(8,128)(2,1)S(1)}, bf16[48,96]{1,0:T(8,128)(2,1)}, u32[]{:S(2)}) copy-start(bf16[48,96]{1,0:T(8,128)(2,1)} %param.13) | copy-start | bytes 27652
  0.0 25.7 %copy-start.1 = (bf16[48,96]{1,0:T(8,128)(2,1)S(1)}, bf16[48,96]{1,0:T(8,128)(2,1)}, u32[]{:S(2)}) copy-start(bf16[48,96]{1,0:T(8,128)(2,1)} %param.12) | copy-start | bytes 27652
  5.7 34.2 %all-to-all-start = ((bf16[48,8,128]{2,1,0:T(8,128)(2,1)}), bf16[48,8,128]{2,1,0:T(8,128)(2,1)S(1)}, u32[]{:S(2)}, u32[]{:S(2)}) async-start(bf16[48,8,128]{2,1,0:T(8,128)(2,1)} %bitcast.5), calls=%async_computation | async-start | bytes 196608 | tf_op jit(solution)/shard_map/all_to_all | solution.py:232
  61.8 28.8 %all-to-all-start.2 = ((bf16[8,384,128]{2,1,0:T(8,128)(2,1)}), bf16[8,384,128]{2,1,0:T(8,128)(2,1)S(1)}, u32[]{:S(2)}, u32[]{:S(2)}) async-start(bf16[8,384,128]{2,1,0:T(8,128)(2,1)} %broadcast_in_dim.8), calls=%async_computation.2 | async-start | bytes 1572864 | tf_op jit(solution)/shard_map/all_to_all | solution.py:235
  73.2 5.6 %collective-permute-start = (bf16[1,400,128]{2,1,0:T(8,128)(2,1)}, bf16[1,400,128]{2,1,0:T(8,128)(2,1)S(1)}, u32[]{:S(2)}, u32[]{:S(2)}) collective-permute-start(bf16[1,400,128]{2,1,0:T(8,128)(2,1)} %get-tuple-element.12), channel_id=1, source_target_pairs={{0,2},{1,3},{2,0},{3,1},{4,6},{5,7},{6,4},{7,5},{8,10},{9,11},{10,... | collective-permute-start | bytes 307208 | tf_op jit(solution)/shard_map/ppermute | solution.py:240
  79.7 8.0 %collective-permute-start.1 = (bf16[2,400,128]{2,1,0:T(8,128)(2,1)S(1)}, bf16[2,400,128]{2,1,0:T(8,128)(2,1)S(1)}, u32[]{:S(2)}, u32[]{:S(2)}) collective-permute-start(bf16[2,400,128]{2,1,0:T(8,128)(2,1)S(1)} %pad_maximum_fusion), channel_id=1, source_target_pairs={{0,8},{1,9},{2,10},{3,11},{4,12},{5,13},{6,14},{7,15},{8,0},{9,1},... | collective-permute-start | bytes 614408 | tf_op jit(solution)/shard_map/ppermute | solution.py:240
  87.7 14.5 %collective-permute-start.2 = (bf16[4,400,128]{2,1,0:T(8,128)(2,1)S(1)}, bf16[4,400,128]{2,1,0:T(8,128)(2,1)S(1)}, u32[]{:S(2)}, u32[]{:S(2)}) collective-permute-start(bf16[4,400,128]{2,1,0:T(8,128)(2,1)S(1)} %constant_dynamic-update-slice_fusion.k0_ref), channel_id=1, source_target_pairs={{0,4},{1,5},{2,6},{3,7},{4,0},{5,1},{6,2},{7,3},{8,12},{9,13},{10,... | collective-permute-start | bytes 1228808 | tf_op jit(solution)/shard_map/ppermute | solution.py:240
  90.6 22.4 %collective-permute-start.5 = (bf16[8,384,128]{2,1,0:T(8,128)(2,1)S(1)}, bf16[8,384,128]{2,1,0:T(8,128)(2,1)S(1)}, u32[]{:S(2)}, u32[]{:S(2)}) collective-permute-start(bf16[8,384,128]{2,1,0:T(8,128)(2,1)S(1)} %all-to-all-done.2.v0_ref), channel_id=1, source_target_pairs={{0,1},{1,0},{2,3},{3,2},{4,5},{5,4},{6,7},{7,6},{8,9},{9,8},{10,11... | collective-permute-start | bytes 2359304 | tf_op jit(solution)/shard_map/ppermute | solution.py:240
  100.3 7.7 %collective-permute-start.3 = (bf16[4,400,128]{2,1,0:T(8,128)(2,1)S(1)}, bf16[4,400,128]{2,1,0:T(8,128)(2,1)S(1)}, u32[]{:S(2)}, u32[]{:S(2)}) collective-permute-start(bf16[4,400,128]{2,1,0:T(8,128)(2,1)S(1)} %constant_dynamic-update-slice_fusion.k0_ref), channel_id=1, source_target_pairs={{0,1},{1,0},{2,3},{3,2},{4,5},{5,4},{6,7},{7,6},{8,9},{9,8},{10,11... | collective-permute-start | bytes 1228808 | tf_op jit(solution)/shard_map/ppermute | solution.py:240
  102.2 6.4 %collective-permute-start.4 = (bf16[4,400,128]{2,1,0:T(8,128)(2,1)S(1)}, bf16[4,400,128]{2,1,0:T(8,128)(2,1)S(1)}, u32[]{:S(2)}, u32[]{:S(2)}) collective-permute-start(bf16[4,400,128]{2,1,0:T(8,128)(2,1)S(1)} %collective-permute-done.2.k1_ref), channel_id=1, source_target_pairs={{0,1},{1,0},{2,3},{3,2},{4,5},{5,4},{6,7},{7,6},{8,9},{9,8},{10,11... | collective-permute-start | bytes 1228808 | tf_op jit(solution)/shard_map/ppermute | solution.py:240

commit v2 on v1

v2 whole, which is shorter than its diff:
```python
import jax
import jax.numpy as jnp
from jax import lax
from jax.experimental import pallas as pl
from jax.experimental.pallas import tpu as pltpu
from jax.sharding import PartitionSpec as P


HEAD_DIM = 128
BLK = 96
PAD = 16
CHUNKS = 8
CORE_GROUPS = [[2 * k + core for k in range(8)] for core in range(2)]
VMEM = pltpu.MemorySpace.VMEM
SMEM = pltpu.MemorySpace.SMEM
HBM = pltpu.MemorySpace.HBM
GRANT = pltpu.CompilerParams(vmem_limit_bytes=16 * 2**20)


def on_chip(x):
    return pltpu.with_memory_space_constraint(x, VMEM)


def off_chip(x):
    return pltpu.with_memory_space_constraint(x, HBM)


def in_vmem(shape, dtype):
    return pltpu.VMEM(shape, dtype)


def product(refs, held, sems):
    width = held[0].shape[1]
    depth = width // CHUNKS

    def copies(k):
        at = pl.ds(k * depth, depth)
        return [
            pltpu.make_async_copy(
                ref.at[:, at] if n == 0 else ref.at[at, :],
                keep.at[:, at] if n == 0 else keep.at[at, :],
                sems.at[n, k],
            )
            for n, (ref, keep) in enumerate(zip(refs, held))
        ]

    for k in range(CHUNKS):
        for copy in copies(k):
            copy.start()
    total = None
    for k in range(CHUNKS):
        for copy in copies(k):
            copy.wait()
        at = slice(k * depth, (k + 1) * depth)
        sides = [keep[at, :] for keep in held[1:]]
        side = sides[0] if len(sides) == 1 else jnp.concatenate(sides, axis=1)
        part = jnp.dot(held[0][:, at], side, preferred_element_type=jnp.float32)
        total = part if total is None else total + part
    return total


def value_kernel(x_ref, w_ref, out_ref, x_held, w_held, sems):
    out_ref[...] = product([x_ref, w_ref], [x_held, w_held], sems).astype(out_ref.dtype)


def project_values(tokens, w_value):
    rows = tokens.shape[0]
    cols = w_value.shape[1]
    return pl.pallas_call(
        value_kernel,
        in_specs=[pl.BlockSpec(memory_space=HBM)] * 2,
        out_specs=pl.BlockSpec(memory_space=VMEM),
        out_shape=in_vmem((rows, cols), jnp.bfloat16),
        scratch_shapes=[
            pltpu.VMEM(tokens.shape, jnp.bfloat16),
            pltpu.VMEM(w_value.shape, jnp.bfloat16),
            pltpu.SemaphoreType.DMA((2, CHUNKS)),
        ],
        compiler_params=GRANT,
        name="project_values",
    )(off_chip(tokens), off_chip(w_value))


def query_key_kernel(ids_ref, x_ref, wq_ref, wk_ref, q_ref, k_ref, x_held, q_held, k_held, sems):
    rows, cols = q_ref.shape
    total = product([x_ref, wq_ref, wk_ref], [x_held, q_held, k_held], sems)
    q_ref[...] = total[:, :cols].astype(q_ref.dtype)
    k_ref[0, :rows, :] = total[:, cols:].astype(k_ref.dtype)
    row = lax.broadcasted_iota(jnp.int32, (PAD, cols), 0)
    ids = jnp.zeros((PAD, cols), jnp.float32)
    for j in range(4):
        ids = jnp.where(row == j, ids_ref[j].astype(jnp.float32), ids)
    k_ref[0, rows:, :] = ids.astype(k_ref.dtype)


def project_queries_keys(block_ids, tokens, w_query, w_key):
    rows = tokens.shape[0]
    cols = w_query.shape[1]
    return pl.pallas_call(
        query_key_kernel,
        in_specs=[pl.BlockSpec(memory_space=SMEM)] + [pl.BlockSpec(memory_space=HBM)] * 3,
        out_specs=[pl.BlockSpec(memory_space=VMEM)] * 2,
        out_shape=[
            pltpu.HBM((rows, cols), jnp.bfloat16),
            in_vmem((1, rows + PAD, cols), jnp.bfloat16),
        ],
        scratch_shapes=[
            pltpu.VMEM(tokens.shape, jnp.bfloat16),
            pltpu.VMEM(w_query.shape, jnp.bfloat16),
            pltpu.VMEM(w_key.shape, jnp.bfloat16),
            pltpu.SemaphoreType.DMA((3, CHUNKS)),
        ],
        compiler_params=GRANT,
        name="project_queries_keys",
    )(block_ids, off_chip(tokens), off_chip(w_query), off_chip(w_key))


def mix_kernel(u_ref, w_in_ref, w_out_ref, out_ref, wide_ref):
    count = u_ref.shape[1]
    hidden_units = w_in_ref.shape[0] // 2
    wide_ref[...] = u_ref[...].astype(jnp.float32)
    flat = jnp.concatenate([wide_ref[:, t, :] for t in range(count)], axis=1)
    parts = jnp.dot(w_in_ref[...], flat.astype(jnp.bfloat16), preferred_element_type=jnp.float32)
    hidden = (jax.nn.silu(parts[:hidden_units]) * parts[hidden_units:]).astype(jnp.bfloat16)
    mixed = flat + jnp.dot(w_out_ref[...], hidden, preferred_element_type=jnp.float32)
    for t in range(count):
        wide_ref[:, t, :] = mixed[:, t * HEAD_DIM : (t + 1) * HEAD_DIM]
    out_ref[...] = wide_ref[...].astype(out_ref.dtype)


def mix(gathered, w_in, w_out):
    return pl.pallas_call(
        mix_kernel,
        in_specs=[pl.BlockSpec(memory_space=VMEM)] * 3,
        out_specs=pl.BlockSpec(memory_space=VMEM),
        out_shape=in_vmem(gathered.shape, jnp.bfloat16),
        scratch_shapes=[pltpu.VMEM(gathered.shape, jnp.float32)],
        compiler_params=GRANT,
        name="mix_heads",
    )(on_chip(gathered), w_in, w_out)


def weight_kernel(ids_ref, q_ref, *refs):
    *key_refs, w_ref, total_ref, s_ref = refs
    half = q_ref.shape[0] // 2
    rows = q_ref.shape[0]
    chunk = 2 * half
    scale = HEAD_DIM ** (-0.5)
    q_row = lax.broadcasted_iota(jnp.int32, (half, 1), 0)
    lane = lax.broadcasted_iota(jnp.int32, (1, chunk), 1)
    lane_off = lane % BLK
    lane_blk = lane // BLK
    sources = [(k_ref, d) for k_ref in key_refs for d in range(k_ref.shape[0])]
    for s in range(2):
        id_lo, id_hi = ids_ref[2 * s], ids_ref[2 * s + 1]
        q_pos = jnp.where(q_row < BLK, id_lo * BLK + q_row, id_hi * BLK + q_row - BLK)
        queries = q_ref[s * half : (s + 1) * half, :]
        top = jnp.full((half, chunk), -1e30, jnp.float32)
        at = 0
        for first in range(0, len(sources), 2):
            pair = sources[first : first + 2]
            keys = jnp.concatenate(
                [k_ref[d, s * half : (s + 1) * half, :] for k_ref, d in pair], axis=0
            )
            k_ids = jnp.zeros((1, chunk), jnp.float32)
            for e, (k_ref, d) in enumerate(pair):
                tail = k_ref[d, rows:, :].astype(jnp.float32)
                for j in range(2):
                    wide = jnp.concatenate([tail[2 * s + j : 2 * s + j + 1, :]] * 3, axis=1)
                    k_ids = jnp.where(lane_blk == 2 * e + j, wide, k_ids)
            k_pos = k_ids.astype(jnp.int32) * BLK + lane_off
            scores = (
                lax.dot_general(
                    queries, keys, (((1,), (1,)), ((), ())), preferred_element_type=jnp.float32
                )
                * scale
            )
            scores = jnp.where(k_pos <= q_pos, scores, -1e30)
            s_ref[:, at : at + chunk] = scores
            top = jnp.maximum(top, scores)
            at += chunk
        top = jnp.max(top, axis=1, keepdims=True)
        total = jnp.zeros((half, chunk), jnp.float32)
        for at in range(0, s_ref.shape[1], chunk):
            weights = jnp.exp(s_ref[:, at : at + chunk] - top)
            total = total + weights
            w_ref[s, :, at : at + chunk] = weights.astype(w_ref.dtype)
        total = jnp.sum(total, axis=1, keepdims=True)
        total_ref[s * half : (s + 1) * half, :] = jnp.broadcast_to(total, (half, HEAD_DIM))


def attention_weights(block_ids, queries, keys):
    rows = queries.shape[0]
    half = rows // 2
    count = sum(piece.shape[0] for piece in keys) * half
    return pl.pallas_call(
        weight_kernel,
        in_specs=[pl.BlockSpec(memory_space=SMEM)]
        + [pl.BlockSpec(memory_space=VMEM)] * (1 + len(keys)),
        out_specs=[pl.BlockSpec(memory_space=VMEM)] * 2,
        out_shape=[
            in_vmem((2, half, count), jnp.bfloat16),
            pltpu.HBM((rows, HEAD_DIM), jnp.float32),
        ],
        scratch_shapes=[pltpu.VMEM((half, count), jnp.float32)],
        compiler_params=GRANT,
        name="attention_weights",
    )(block_ids, off_chip(queries), *keys)


def summed(spot_ref, w_ref, v_ref, s, first):
    half = w_ref.shape[1]
    sources = 4
    acc = jnp.zeros((half, HEAD_DIM), jnp.float32)
    for d in range(0, v_ref.shape[0], sources):
        values = jnp.concatenate(
            [v_ref[spot_ref[d + e], s * half : (s + 1) * half, :] for e in range(sources)], axis=0
        )
        at = first + d * half
        acc = acc + jnp.dot(
            w_ref[s, :, at : at + sources * half], values, preferred_element_type=jnp.float32
        )
    return acc


def first_kernel(spot_ref, w_ref, v_ref, part_ref):
    half = w_ref.shape[1]
    for s in range(2):
        part_ref[s * half : (s + 1) * half, :] = summed(spot_ref, w_ref, v_ref, s, 0)


def last_kernel(spot_ref, w_ref, total_ref, part_ref, v_ref, out_ref):
    half = w_ref.shape[1]
    for s in range(2):
        rows = slice(s * half, (s + 1) * half)
        acc = part_ref[rows, :] + summed(spot_ref, w_ref, v_ref, s, w_ref.shape[2] // 2)
        out_ref[rows, :] = (acc / total_ref[rows, :]).astype(out_ref.dtype)


def apply_first(spots, weights, values):
    rows = values.shape[1]
    return pl.pallas_call(
        first_kernel,
        in_specs=[pl.BlockSpec(memory_space=SMEM)] + [pl.BlockSpec(memory_space=VMEM)] * 2,
        out_specs=pl.BlockSpec(memory_space=VMEM),
        out_shape=in_vmem((rows, HEAD_DIM), jnp.float32),
        compiler_params=GRANT,
        name="apply_first",
    )(spots, weights, on_chip(values))


def apply_last(spots, weights, total, part, values):
    return pl.pallas_call(
        last_kernel,
        in_specs=[pl.BlockSpec(memory_space=SMEM)] + [pl.BlockSpec(memory_space=VMEM)] * 4,
        out_specs=pl.BlockSpec(memory_space=VMEM),
        out_shape=jax.ShapeDtypeStruct(total.shape, jnp.bfloat16),
        compiler_params=GRANT,
        name="apply_last",
    )(spots, weights, off_chip(total), part, on_chip(values))


def pack_kernel(*refs):
    *pieces, out_ref = refs
    for n in range(out_ref.shape[0]):
        out_ref[n] = pieces[n % len(pieces)][0]


def pack(count, *pieces):
    return pl.pallas_call(
        pack_kernel,
        in_specs=[pl.BlockSpec(memory_space=VMEM)] * len(pieces),
        out_specs=pl.BlockSpec(memory_space=VMEM),
        out_shape=in_vmem((count, *pieces[0].shape[1:]), pieces[0].dtype),
        compiler_params=GRANT,
        name="pack",
    )(*[on_chip(piece) for piece in pieces])


def shards(tokens, w_query, w_key, w_value, mix_gate, mix_up, mix_down, block_ids):
    heads = mix_gate.shape[0]
    rows = tokens.shape[0]

    def exchange(x):
        return lax.all_to_all(x, "tensor", split_axis=0, concat_axis=0, tiled=True)

    def spread(x):
        return lax.all_to_all(
            x, "context", split_axis=0, concat_axis=0, axis_index_groups=CORE_GROUPS, tiled=True
        )

    def flip(x, bit):
        return lax.ppermute(x, "context", [(i, i ^ bit) for i in range(16)])

    w_in = jnp.concatenate([mix_gate, mix_up], axis=1).T
    w_out = mix_down.T
    values = project_values(tokens, w_value)
    gathered = exchange(values.reshape(heads, rows // heads, HEAD_DIM))
    tokens, values = lax.optimization_barrier((tokens, values))
    queries, own = project_queries_keys(block_ids, tokens, w_query, w_key)
    beside = flip(own, 2)
    far = flip(own, 8)
    mixed = mix(gathered, w_in, w_out)
    mixed_rows = exchange(mixed).reshape(1, rows, HEAD_DIM)
    far_beside = flip(far, 2)
    quad = pack(4, own, beside, far, far_beside)
    near = flip(quad, 4)
    keys = [quad, near, flip(quad, 1), flip(near, 1)]
    turn = jnp.arange(8, dtype=jnp.int32)
    spots = (lax.axis_index("context") // 2) ^ (turn % 2 + turn // 2 % 2 * 4 + turn // 4 * 2)
    weights, total = attention_weights(block_ids, queries, keys)
    copies = pack(8, mixed_rows)
    values_mine = spread(copies)
    values_other = flip(values_mine, 1)
    part = apply_first(spots, weights, values_mine)
    return apply_last(spots, weights, total, part, values_other)


def solution(mesh):
    in_specs = (
        P("context", None),
        P(None, "tensor"),
        P(None, "tensor"),
        P(None, "tensor"),
        P(),
        P(),
        P(),
        P("context"),
    )
    out_specs = P("context", "tensor")
    return jax.shard_map(shards, mesh=mesh, in_specs=in_specs, out_specs=out_specs, check_vma=False)
```

time: 117 us -> 112 us (0.957)
  the two profiles are of different devices: /device:TPU:13 before, /device:TPU:1 now
where the time goes in v2:
time: 112 us; the launch traced here: 111 us
  starting transfers between devices  53.6 us (48%)
  Pallas kernels  21 us (19%)
  waiting for transfers between devices  18.5 us (17%)
  blocking collectives  18 us (16%)
    ppermute x7, starting transfers between devices, flip(): return lax.ppermute(x, 'context', [(i, i ^ bit) for i in range(16)])  27.7 us
    all_to_all x1, starting transfers between devices, exchange(): return lax.all_to_all(x, 'tensor', split_axis=0, concat_axis=0, tiled=True)  21.6 us
    all_to_all x1, blocking collectives, exchange(): return lax.all_to_all(x, 'tensor', split_axis=0, concat_axis=0, tiled=True)  18 us
    all_to_all x1, waiting for transfers between devices, exchange(): return lax.all_to_all(x, 'tensor', split_axis=0, concat_axis=0, tiled=True)  14 us
    pallas_call x1, Pallas kernels, project_queries_keys(): pl.pallas_call(query_key_kernel, in_specs=[pl.BlockSpec(memory_space=SMEM...  6.79 us
    pallas_call x1, Pallas kernels, project_values(): pl.pallas_call(value_kernel, in_specs=[pl.BlockSpec(memory_space=HBM)] *...  6.04 us
    ppermute x7, waiting for transfers between devices, flip(): return lax.ppermute(x, 'context', [(i, i ^ bit) for i in range(16)])  4.45 us
    all_to_all x1, starting transfers between devices, spread(): lax.all_to_all(x, 'context', split_axis=0, concat_axis=0, axis_index_grou...  4.17 us
  transfers between devices with their start and end apart: 9, of which 4 were waited for; matrix products, arithmetic and copies ran while one was open for 0% of the time, Pallas kernels for 10%

profile of v2, /device:TPU:1, one launch (start us, length us, event | category | flops | bytes accessed | tf_op | source)
XLA Modules:
  0.0 111.5 jit_solution(11320203989425937838)
XLA Ops:
  0.0 0.0 copy-start.2
  0.0 0.0 copy-start.3
  0.0 0.0 copy-start
  0.0 6.0 %project_values.1 = bf16[384,128]{1,0:T(8,128)(2,1)} custom-call(bf16[384,8192]{1,0:T(8,128)(2,1)} %x_ref.2, bf16[8192,128]{1,0:T(8,128)(2,1)} %w_ref.1), custom_call_target="tpu_custom_call" | custom-call | tf_op jit(solution)/shard_map/project_values/pallas_call | solution.py:69
  6.1 0.0 copy-start.1
  6.1 21.6 %all-to-all-start = ((bf16[48,8,128]{2,1,0:T(8,128)(2,1)}), bf16[48,8,128]{2,1,0:T(8,128)(2,1)S(1)}, u32[]{:S(2)}, u32[]{:S(2)}) async-start(bf16[48,8,128]{2,1,0:T(8,128)(2,1)} %bitcast), calls=%async_computation | async-start | bytes 196608 | tf_op jit(solution)/shard_map/all_to_all | solution.py:285
  27.7 0.0 copy-done.2
  27.7 0.1 copy.10
  27.8 0.0 copy-done.3
  27.8 0.1 copy.9
  28.0 14.0 %all-to-all-done.u_ref = bf16[48,8,128]{2,1,0:T(8,128)(2,1)S(1)} async-done(((bf16[48,8,128]{2,1,0:T(8,128)(2,1)}), bf16[48,8,128]{2,1,0:T(8,128)(2,1)S(1)}, u32[]{:S(2)}, u32[]{:S(2)}) %all-to-all-start) | async-done | bytes 98336 | tf_op jit(solution)/shard_map/all_to_all | solution.py:285
  42.0 0.0 copy-done
  42.0 0.5 mix_heads.1
  42.5 18.0 %all_to_all.15 = bf16[48,8,128]{2,1,0:T(8,128)(2,1)S(1)} all-to-all(bf16[48,8,128]{2,1,0:T(8,128)(2,1)S(1)} %mix_heads.1), channel_id=1, replica_groups=mesh['tensor'=48,'context'=16] {'tensor'}, dimensions={0} | all-to-all | bytes 196608 | tf_op jit(solution)/shard_map/all_to_all | solution.py:285
  60.5 1.0 pack.3
  61.5 4.2 %all-to-all-start.2 = ((bf16[8,384,128]{2,1,0:T(8,128)(2,1)}), bf16[8,384,128]{2,1,0:T(8,128)(2,1)S(1)}, u32[]{:S(2)}, u32[]{:S(2)}) async-start(bf16[8,384,128]{2,1,0:T(8,128)(2,1)} %pack.3), calls=%async_computation.2 | async-start | bytes 1572864 | tf_op jit(solution)/shard_map/all_to_all | solution.py:288
  65.7 0.0 copy-done.1
  65.7 6.8 %project_queries_keys.1 = (bf16[384,128]{1,0:T(8,128)(2,1)}, bf16[1,400,128]{2,1,0:T(8,128)(2,1)S(1)}) custom-call(s32[4]{0:T(128)S(1)} %copy-done.1, bf16[384,8192]{1,0:T(8,128)(2,1)} %x_ref.2, bf16[8192,128]{1,0:T(8,128)(2,1)} %wq_ref.1, bf16[8192,128]{1,0:T(8,128)(2,1)} %wk_ref.1), custom_call_target="tpu_custom_call" | custom-call | tf_op jit(solution)/shard_map/project_queries_keys/pallas_call | solution.py:99
  72.5 4.9 %collective-permute-start.1 = (bf16[1,400,128]{2,1,0:T(8,128)(2,1)S(1)}, bf16[1,400,128]{2,1,0:T(8,128)(2,1)S(1)}, u32[]{:S(2)}, u32[]{:S(2)}) collective-permute-start(bf16[1,400,128]{2,1,0:T(8,128)(2,1)S(1)} %get-tuple-element.12.refs_0_), channel_id=1, source_target_pairs={{0,8},{1,9},{2,10},{3,11},{4,12},{5,13},{6,14},{7,15},{8,0},{9,1},... | collective-permute-start | bytes 307208 | tf_op jit(solution)/shard_map/ppermute | solution.py:293
  77.4 3.1 %collective-permute-start = (bf16[1,400,128]{2,1,0:T(8,128)(2,1)S(1)}, bf16[1,400,128]{2,1,0:T(8,128)(2,1)S(1)}, u32[]{:S(2)}, u32[]{:S(2)}) collective-permute-start(bf16[1,400,128]{2,1,0:T(8,128)(2,1)S(1)} %get-tuple-element.12.refs_0_), channel_id=1, source_target_pairs={{0,2},{1,3},{2,0},{3,1},{4,6},{5,7},{6,4},{7,5},{8,10},{9,11},{10,... | collective-permute-start | bytes 307208 | tf_op jit(solution)/shard_map/ppermute | solution.py:293
  80.5 0.0 collective-permute-done.1.refs_2_
  80.5 2.3 %collective-permute-start.2 = (bf16[1,400,128]{2,1,0:T(8,128)(2,1)S(1)}, bf16[1,400,128]{2,1,0:T(8,128)(2,1)S(1)}, u32[]{:S(2)}, u32[]{:S(2)}) collective-permute-start(bf16[1,400,128]{2,1,0:T(8,128)(2,1)S(1)} %collective-permute-done.1.refs_2_), channel_id=1, source_target_pairs={{0,2},{1,3},{2,0},{3,1},{4,6},{5,7},{6,4},{7,5},{8,10},{9,11},{10,... | collective-permute-start | bytes 307208 | tf_op jit(solution)/shard_map/ppermute | solution.py:293
  82.8 0.3 collective-permute-done.refs_1_
  83.1 2.8 %collective-permute-done.2.refs_3_ = bf16[1,400,128]{2,1,0:T(8,128)(2,1)S(1)} collective-permute-done((bf16[1,400,128]{2,1,0:T(8,128)(2,1)S(1)}, bf16[1,400,128]{2,1,0:T(8,128)(2,1)S(1)}, u32[]{:S(2)}, u32[]{:S(2)}) %collective-permute-start.2) | collective-permute-done | bytes 102432 | tf_op jit(solution)/shard_map/ppermute | solution.py:293
  85.9 2.3 %collective-permute-start.3 = (bf16[4,400,128]{2,1,0:T(8,128)(2,1)S(1)}, bf16[4,400,128]{2,1,0:T(8,128)(2,1)S(1)}, u32[]{:S(2)}, u32[]{:S(2)}) collective-permute-start(bf16[4,400,128]{2,1,0:T(8,128)(2,1)S(1)} %pack.2.refs_0_), channel_id=1, source_target_pairs={{0,4},{1,5},{2,6},{3,7},{4,0},{5,1},{6,2},{7,3},{8,12},{9,13},{10,... | collective-permute-start | bytes 1228808 | tf_op jit(solution)/shard_map/ppermute | solution.py:293
  88.2 0.0 all-to-all-done.2.v_ref
  88.2 8.6 %collective-permute-start.6 = (bf16[8,384,128]{2,1,0:T(8,128)(2,1)S(1)}, bf16[8,384,128]{2,1,0:T(8,128)(2,1)S(1)}, u32[]{:S(2)}, u32[]{:S(2)}) collective-permute-start(bf16[8,384,128]{2,1,0:T(8,128)(2,1)S(1)} %all-to-all-done.2.v_ref), channel_id=1, source_target_pairs={{0,1},{1,0},{2,3},{3,2},{4,5},{5,4},{6,7},{7,6},{8,9},{9,8},{10,11... | collective-permute-start | bytes 2359304 | tf_op jit(solution)/shard_map/ppermute | solution.py:293
  96.8 1.9 %collective-permute-start.4 = (bf16[4,400,128]{2,1,0:T(8,128)(2,1)S(1)}, bf16[4,400,128]{2,1,0:T(8,128)(2,1)S(1)}, u32[]{:S(2)}, u32[]{:S(2)}) collective-permute-start(bf16[4,400,128]{2,1,0:T(8,128)(2,1)S(1)} %pack.2.refs_0_), channel_id=1, source_target_pairs={{0,1},{1,0},{2,3},{3,2},{4,5},{5,4},{6,7},{7,6},{8,9},{9,8},{10,11... | collective-permute-start | bytes 1228808 | tf_op jit(solution)/shard_map/ppermute | solution.py:293
  98.8 0.0 collective-permute-done.3.refs_1_
  98.8 4.7 %collective-permute-start.5 = (bf16[4,400,128]{2,1,0:T(8,128)(2,1)S(1)}, bf16[4,400,128]{2,1,0:T(8,128)(2,1)S(1)}, u32[]{:S(2)}, u32[]{:S(2)}) collective-permute-start(bf16[4,400,128]{2,1,0:T(8,128)(2,1)S(1)} %collective-permute-done.3.refs_1_), channel_id=1, source_target_pairs={{0,1},{1,0},{2,3},{3,2},{4,5},{5,4},{6,7},{7,6},{8,9},{9,8},{10,11... | collective-permute-start | bytes 1228808 | tf_op jit(solution)/shard_map/ppermute | solution.py:293
  103.5 0.0 collective-permute-done.4.refs_2_
  103.5 1.3 %collective-permute-done.5.refs_3_ = bf16[4,400,128]{2,1,0:T(8,128)(2,1)S(1)} collective-permute-done((bf16[4,400,128]{2,1,0:T(8,128)(2,1)S(1)}, bf16[4,400,128]{2,1,0:T(8,128)(2,1)S(1)}, u32[]{:S(2)}, u32[]{:S(2)}) %collective-permute-start.5) | collective-permute-done | bytes 409632 | tf_op jit(solution)/shard_map/ppermute | solution.py:293
  104.9 3.5 %attention_weights.1 = (bf16[2,192,3072]{2,1,0:T(8,128)(2,1)S(1)}, f32[384,128]{1,0:T(8,128)}) custom-call(s32[4]{0:T(128)S(1)} %copy-done.1, bf16[384,128]{1,0:T(8,128)(2,1)} %get-tuple-element.11.q_ref, bf16[4,400,128]{2,1,0:T(8,128)(2,1)S(1)} %pack.2.refs_0_, bf16[4,400,128]{2,1,0:T(8,128)(2,1)S(1)} %collective-permute-done.3.refs_1_, ...), custom_call_target="tpu_custom_call" | custom-call | tf_op jit(solution)/shard_map/attention_weights/pallas_call | solution.py:196
  108.4 1.0 apply_first.1.part_ref
  109.4 0.0 collective-permute-done.6.v_ref
  109.4 2.0 %apply_last.1 = bf16[384,128]{1,0:T(8,128)(2,1)} custom-call(s32[8]{0:T(128)S(1)} %fusion.3.spot_ref, bf16[2,192,3072]{2,1,0:T(8,128)(2,1)S(1)} %get-tuple-element.13.w_ref, f32[384,128]{1,0:T(8,128)} %get-tuple-element.14.total_ref, f32[384,128]{1,0:T(8,128)S(1)} %apply_first.1.part_ref, bf16[8,384,128]{2,1,0:T(8,128)(2,1)S(1)} %collective-permute-done.6.v_ref), custom_call_target="tpu_custom_call" | custom-call | tf_op jit(solution)/shard_map/apply_last/pallas_call | solution.py:253
  (3 shorter events, 0.1 us)
Async XLA Ops:
  0.0 27.7 %copy-start.2 = (bf16[48,96]{1,0:T(8,128)(2,1)S(1)}, bf16[48,96]{1,0:T(8,128)(2,1)}, u32[]{:S(2)}) copy-start(bf16[48,96]{1,0:T(8,128)(2,1)} %param.13) | copy-start | bytes 27652
  0.0 27.8 %copy-start.3 = (bf16[48,96]{1,0:T(8,128)(2,1)S(1)}, bf16[48,96]{1,0:T(8,128)(2,1)}, u32[]{:S(2)}) copy-start(bf16[48,96]{1,0:T(8,128)(2,1)} %param.12) | copy-start | bytes 27652
  0.0 42.0 %copy-start = (bf16[96,48]{0,1:T(8,128)(2,1)S(1)}, bf16[96,48]{0,1:T(8,128)(2,1)}, u32[]{:S(2)}) copy-start(bf16[96,48]{0,1:T(8,128)(2,1)} %param.14) | copy-start | bytes 27652
  6.1 59.7 %copy-start.1 = (s32[4]{0:T(128)S(1)}, s32[4]{0:T(128)}, u32[]{:S(2)}) copy-start(s32[4]{0:T(128)} %ids_ref.3) | copy-start | bytes 52
  6.1 35.9 %all-to-all-start = ((bf16[48,8,128]{2,1,0:T(8,128)(2,1)}), bf16[48,8,128]{2,1,0:T(8,128)(2,1)S(1)}, u32[]{:S(2)}, u32[]{:S(2)}) async-start(bf16[48,8,128]{2,1,0:T(8,128)(2,1)} %bitcast), calls=%async_computation | async-start | bytes 196608 | tf_op jit(solution)/shard_map/all_to_all | solution.py:285
  61.5 26.7 %all-to-all-start.2 = ((bf16[8,384,128]{2,1,0:T(8,128)(2,1)}), bf16[8,384,128]{2,1,0:T(8,128)(2,1)S(1)}, u32[]{:S(2)}, u32[]{:S(2)}) async-start(bf16[8,384,128]{2,1,0:T(8,128)(2,1)} %pack.3), calls=%async_computation.2 | async-start | bytes 1572864 | tf_op jit(solution)/shard_map/all_to_all | solution.py:288
  72.5 8.0 %collective-permute-start.1 = (bf16[1,400,128]{2,1,0:T(8,128)(2,1)S(1)}, bf16[1,400,128]{2,1,0:T(8,128)(2,1)S(1)}, u32[]{:S(2)}, u32[]{:S(2)}) collective-permute-start(bf16[1,400,128]{2,1,0:T(8,128)(2,1)S(1)} %get-tuple-element.12.refs_0_), channel_id=1, source_target_pairs={{0,8},{1,9},{2,10},{3,11},{4,12},{5,13},{6,14},{7,15},{8,0},{9,1},... | collective-permute-start | bytes 307208 | tf_op jit(solution)/shard_map/ppermute | solution.py:293
  77.4 5.7 %collective-permute-start = (bf16[1,400,128]{2,1,0:T(8,128)(2,1)S(1)}, bf16[1,400,128]{2,1,0:T(8,128)(2,1)S(1)}, u32[]{:S(2)}, u32[]{:S(2)}) collective-permute-start(bf16[1,400,128]{2,1,0:T(8,128)(2,1)S(1)} %get-tuple-element.12.refs_0_), channel_id=1, source_target_pairs={{0,2},{1,3},{2,0},{3,1},{4,6},{5,7},{6,4},{7,5},{8,10},{9,11},{10,... | collective-permute-start | bytes 307208 | tf_op jit(solution)/shard_map/ppermute | solution.py:293
  80.5 5.4 %collective-permute-start.2 = (bf16[1,400,128]{2,1,0:T(8,128)(2,1)S(1)}, bf16[1,400,128]{2,1,0:T(8,128)(2,1)S(1)}, u32[]{:S(2)}, u32[]{:S(2)}) collective-permute-start(bf16[1,400,128]{2,1,0:T(8,128)(2,1)S(1)} %collective-permute-done.1.refs_2_), channel_id=1, source_target_pairs={{0,2},{1,3},{2,0},{3,1},{4,6},{5,7},{6,4},{7,5},{8,10},{9,11},{10,... | collective-permute-start | bytes 307208 | tf_op jit(solution)/shard_map/ppermute | solution.py:293
  85.9 12.8 %collective-permute-start.3 = (bf16[4,400,128]{2,1,0:T(8,128)(2,1)S(1)}, bf16[4,400,128]{2,1,0:T(8,128)(2,1)S(1)}, u32[]{:S(2)}, u32[]{:S(2)}) collective-permute-start(bf16[4,400,128]{2,1,0:T(8,128)(2,1)S(1)} %pack.2.refs_0_), channel_id=1, source_target_pairs={{0,4},{1,5},{2,6},{3,7},{4,0},{5,1},{6,2},{7,3},{8,12},{9,13},{10,... | collective-permute-start | bytes 1228808 | tf_op jit(solution)/shard_map/ppermute | solution.py:293
  88.2 21.2 %collective-permute-start.6 = (bf16[8,384,128]{2,1,0:T(8,128)(2,1)S(1)}, bf16[8,384,128]{2,1,0:T(8,128)(2,1)S(1)}, u32[]{:S(2)}, u32[]{:S(2)}) collective-permute-start(bf16[8,384,128]{2,1,0:T(8,128)(2,1)S(1)} %all-to-all-done.2.v_ref), channel_id=1, source_target_pairs={{0,1},{1,0},{2,3},{3,2},{4,5},{5,4},{6,7},{7,6},{8,9},{9,8},{10,11... | collective-permute-start | bytes 2359304 | tf_op jit(solution)/shard_map/ppermute | solution.py:293
  96.8 6.7 %collective-permute-start.4 = (bf16[4,400,128]{2,1,0:T(8,128)(2,1)S(1)}, bf16[4,400,128]{2,1,0:T(8,128)(2,1)S(1)}, u32[]{:S(2)}, u32[]{:S(2)}) collective-permute-start(bf16[4,400,128]{2,1,0:T(8,128)(2,1)S(1)} %pack.2.refs_0_), channel_id=1, source_target_pairs={{0,1},{1,0},{2,3},{3,2},{4,5},{5,4},{6,7},{7,6},{8,9},{9,8},{10,11... | collective-permute-start | bytes 1228808 | tf_op jit(solution)/shard_map/ppermute | solution.py:293
  98.8 6.1 %collective-permute-start.5 = (bf16[4,400,128]{2,1,0:T(8,128)(2,1)S(1)}, bf16[4,400,128]{2,1,0:T(8,128)(2,1)S(1)}, u32[]{:S(2)}, u32[]{:S(2)}) collective-permute-start(bf16[4,400,128]{2,1,0:T(8,128)(2,1)S(1)} %collective-permute-done.3.refs_1_), channel_id=1, source_target_pairs={{0,1},{1,0},{2,3},{3,2},{4,5},{5,4},{6,7},{7,6},{8,9},{9,8},{10,11... | collective-permute-start | bytes 1228808 | tf_op jit(solution)/shard_map/ppermute | solution.py:293

commit v3 on v2

--- a/solution.py
+++ b/solution.py
@@ -30,8 +30,9 @@
 
 
 def product(refs, held, sems):
-    width = held[0].shape[1]
+    rows, width = held[0].shape
     depth = width // CHUNKS
+    third = rows // 3
 
     def copies(k):
         at = pl.ds(k * depth, depth)
@@ -47,16 +48,19 @@
     for k in range(CHUNKS):
         for copy in copies(k):
             copy.start()
-    total = None
+    totals = [None] * 3
     for k in range(CHUNKS):
         for copy in copies(k):
             copy.wait()
         at = slice(k * depth, (k + 1) * depth)
         sides = [keep[at, :] for keep in held[1:]]
         side = sides[0] if len(sides) == 1 else jnp.concatenate(sides, axis=1)
-        part = jnp.dot(held[0][:, at], side, preferred_element_type=jnp.float32)
-        total = part if total is None else total + part
-    return total
+        for n in range(3):
+            part = jnp.dot(
+                held[0][n * third : (n + 1) * third, at], side, preferred_element_type=jnp.float32
+            )
+            totals[n] = part if totals[n] is None else totals[n] + part
+    return jnp.concatenate(totals, axis=0)
 
 
 def value_kernel(x_ref, w_ref, out_ref, x_held, w_held, sems):
@@ -112,7 +116,7 @@
         ],
         compiler_params=GRANT,
         name="project_queries_keys",
-    )(block_ids, off_chip(tokens), off_chip(w_query), off_chip(w_key))
+    )(off_chip(block_ids), off_chip(tokens), off_chip(w_query), off_chip(w_key))
 
 
 def mix_kernel(u_ref, w_in_ref, w_out_ref, out_ref, wide_ref):
@@ -141,7 +145,14 @@
 
 
 def weight_kernel(ids_ref, q_ref, *refs):
-    *key_refs, w_ref, total_ref, s_ref = refs
+    quad_ref, near_ref, far_quad_ref, far_near_ref, w_ref, total_ref, s_ref, *held, sems = refs
+    copies = [
+        pltpu.make_async_copy(ref, keep, sems.at[n])
+        for n, (ref, keep) in enumerate(zip((near_ref, far_quad_ref), held))
+    ]
+    for copy in copies:
+        copy.start()
+    key_refs = [quad_ref, *held, far_near_ref]
     half = q_ref.shape[0] // 2
     rows = q_ref.shape[0]
     chunk = 2 * half
@@ -159,6 +170,8 @@
         at = 0
         for first in range(0, len(sources), 2):
             pair = sources[first : first + 2]
+            if s == 0 and first in (4, 8):
+                copies[first // 4 - 1].wait()
             keys = jnp.concatenate(
                 [k_ref[d, s * half : (s + 1) * half, :] for k_ref, d in pair], axis=0
             )
@@ -193,28 +206,36 @@
     rows = queries.shape[0]
     half = rows // 2
     count = sum(piece.shape[0] for piece in keys) * half
+    places = [on_chip, off_chip, off_chip, on_chip]
     return pl.pallas_call(
         weight_kernel,
         in_specs=[pl.BlockSpec(memory_space=SMEM)]
-        + [pl.BlockSpec(memory_space=VMEM)] * (1 + len(keys)),
+        + [pl.BlockSpec(memory_space=space) for space in (VMEM, VMEM, HBM, HBM, VMEM)],
         out_specs=[pl.BlockSpec(memory_space=VMEM)] * 2,
         out_shape=[
             in_vmem((2, half, count), jnp.bfloat16),
             pltpu.HBM((rows, HEAD_DIM), jnp.float32),
         ],
-        scratch_shapes=[pltpu.VMEM((half, count), jnp.float32)],
+        scratch_shapes=[
+            pltpu.VMEM((half, count), jnp.float32),
+            pltpu.VMEM(keys[1].shape, jnp.bfloat16),
+            pltpu.VMEM(keys[2].shape, jnp.bfloat16),
+            pltpu.SemaphoreType.DMA((2,)),
+        ],
         compiler_params=GRANT,
         name="attention_weights",
-    )(block_ids, off_chip(queries), *keys)
-
-
-def summed(spot_ref, w_ref, v_ref, s, first):
+    )(off_chip(block_ids), off_chip(queries), *[place(k) for place, k in zip(places, keys)])
+
+
+def summed(w_ref, v_ref, s, first):
     half = w_ref.shape[1]
     sources = 4
+    mine = lax.axis_index("context") // 2
     acc = jnp.zeros((half, HEAD_DIM), jnp.float32)
     for d in range(0, v_ref.shape[0], sources):
+        turns = [e % 2 + e // 2 % 2 * 4 + e // 4 * 2 for e in range(d, d + sources)]
         values = jnp.concatenate(
-            [v_ref[spot_ref[d + e], s * half : (s + 1) * half, :] for e in range(sources)], axis=0
+            [v_ref[mine ^ turn, s * half : (s + 1) * half, :] for turn in turns], axis=0
         )
         at = first + d * half
         acc = acc + jnp.dot(
@@ -223,58 +244,80 @@
     return acc
 
 
-def first_kernel(spot_ref, w_ref, v_ref, part_ref):
+def first_kernel(w_ref, total_ref, v_ref, part_ref, kept_ref):
     half = w_ref.shape[1]
     for s in range(2):
-        part_ref[s * half : (s + 1) * half, :] = summed(spot_ref, w_ref, v_ref, s, 0)
-
-
-def last_kernel(spot_ref, w_ref, total_ref, part_ref, v_ref, out_ref):
+        part_ref[s * half : (s + 1) * half, :] = summed(w_ref, v_ref, s, 0)
+    kept_ref[...] = total_ref[...]
+
+
+def last_kernel(w_ref, total_ref, part_ref, v_ref, out_ref):
     half = w_ref.shape[1]
     for s in range(2):
         rows = slice(s * half, (s + 1) * half)
-        acc = part_ref[rows, :] + summed(spot_ref, w_ref, v_ref, s, w_ref.shape[2] // 2)
+        acc = part_ref[rows, :] + summed(w_ref, v_ref, s, w_ref.shape[2] // 2)
         out_ref[rows, :] = (acc / total_ref[rows, :]).astype(out_ref.dtype)
 
 
-def apply_first(spots, weights, values):
-    rows = values.shape[1]
+def apply_first(weights, total, values):
     return pl.pallas_call(
         first_kernel,
-        in_specs=[pl.BlockSpec(memory_space=SMEM)] + [pl.BlockSpec(memory_space=VMEM)] * 2,
-        out_specs=pl.BlockSpec(memory_space=VMEM),
-        out_shape=in_vmem((rows, HEAD_DIM), jnp.float32),
+        in_specs=[pl.BlockSpec(memory_space=VMEM)] * 3,
+        out_specs=[pl.BlockSpec(memory_space=VMEM)] * 2,
+        out_shape=[in_vmem(total.shape, jnp.float32)] * 2,
         compiler_params=GRANT,
         name="apply_first",
-    )(spots, weights, on_chip(values))
-
-
-def apply_last(spots, weights, total, part, values):
+    )(weights, off_chip(total), on_chip(values))
+
+
+def apply_last(weights, total, part, values):
     return pl.pallas_call(
         last_kernel,
-        in_specs=[pl.BlockSpec(memory_space=SMEM)] + [pl.BlockSpec(memory_space=VMEM)] * 4,
+        in_specs=[pl.BlockSpec(memory_space=VMEM)] * 4,
         out_specs=pl.BlockSpec(memory_space=VMEM),
         out_shape=jax.ShapeDtypeStruct(total.shape, jnp.bfloat16),
         compiler_params=GRANT,
         name="apply_last",
-    )(spots, weights, off_chip(total), part, on_chip(values))
+    )(weights, total, part, on_chip(values))
 
 
 def pack_kernel(*refs):
     *pieces, out_ref = refs
-    for n in range(out_ref.shape[0]):
-        out_ref[n] = pieces[n % len(pieces)][0]
-
-
-def pack(count, *pieces):
+    for n, piece in enumerate(pieces):
+        out_ref[n] = piece[0]
+
+
+def pack(*pieces):
     return pl.pallas_call(
         pack_kernel,
         in_specs=[pl.BlockSpec(memory_space=VMEM)] * len(pieces),
         out_specs=pl.BlockSpec(memory_space=VMEM),
-        out_shape=in_vmem((count, *pieces[0].shape[1:]), pieces[0].dtype),
+        out_shape=in_vmem((len(pieces), *pieces[0].shape[1:]), pieces[0].dtype),
         compiler_params=GRANT,
         name="pack",
     )(*[on_chip(piece) for piece in pieces])
+
+
+def repeat_kernel(x_ref, out_ref, sems):
+    copies = [
+        pltpu.make_async_copy(x_ref, out_ref.at[n], sems.at[n]) for n in range(out_ref.shape[0])
+    ]
+    for copy in copies:
+        copy.start()
+    for copy in copies:
+        copy.wait()
+
+
+def repeat(x, count):
+    return pl.pallas_call(
+        repeat_kernel,
+        in_specs=[pl.BlockSpec(memory_space=VMEM)],
+        out_specs=pl.BlockSpec(memory_space=HBM),
+        out_shape=pltpu.HBM((count, *x.shape), x.dtype),
+        scratch_shapes=[pltpu.SemaphoreType.DMA((count,))],
+        compiler_params=GRANT,
+        name="repeat",
+    )(on_chip(x))
 
 
 def shards(tokens, w_query, w_key, w_value, mix_gate, mix_up, mix_down, block_ids):
@@ -301,19 +344,19 @@
     beside = flip(own, 2)
     far = flip(own, 8)
     mixed = mix(gathered, w_in, w_out)
-    mixed_rows = exchange(mixed).reshape(1, rows, HEAD_DIM)
+    mixed_rows = exchange(mixed).reshape(rows, HEAD_DIM)
     far_beside = flip(far, 2)
-    quad = pack(4, own, beside, far, far_beside)
+    quad = pack(own, beside, far, far_beside)
     near = flip(quad, 4)
-    keys = [quad, near, flip(quad, 1), flip(near, 1)]
-    turn = jnp.arange(8, dtype=jnp.int32)
-    spots = (lax.axis_index("context") // 2) ^ (turn % 2 + turn // 2 % 2 * 4 + turn // 4 * 2)
+    other_quad = flip(quad, 1)
+    other_near = flip(near, 1)
+    keys = [quad, near, other_quad, other_near]
     weights, total = attention_weights(block_ids, queries, keys)
-    copies = pack(8, mixed_rows)
+    copies = repeat(mixed_rows, 8)
     values_mine = spread(copies)
     values_other = flip(values_mine, 1)
-    part = apply_first(spots, weights, values_mine)
-    return apply_last(spots, weights, total, part, values_other)
+    part, total = apply_first(weights, total, values_mine)
+    return apply_last(weights, total, part, values_other)
 
 
 def solution(mesh):

time: 112 us -> 111 us (level)
  Pallas kernels: 21 us -> 19.8 us
    pallas_call x2 -> x3, Pallas kernels: 3.05 us -> 3.48 us  [the longest x1 1.4 us: apply_first(): pl.pallas_call(first_kernel, in_specs=[pl.BlockSpec(memory_space=VMEM)] *...]
  transfers between devices with their start and end apart: 9 -> 9, of which waited for: 4 -> 4; matrix products, arithmetic and copies ran while one was open for 0% -> 0% of each run, Pallas kernels for 10% -> 11%
where the time goes in v3:
time: 111 us; the launch traced here: 110 us
  starting transfers between devices  52.9 us (48%)
  Pallas kernels  19.8 us (18%)
  waiting for transfers between devices  19.1 us (17%)
  blocking collectives  18 us (16%)
    ppermute x7, starting transfers between devices, flip(): return lax.ppermute(x, 'context', [(i, i ^ bit) for i in range(16)])  27.1 us
    all_to_all x1, starting transfers between devices, exchange(): return lax.all_to_all(x, 'tensor', split_axis=0, concat_axis=0, tiled=True)  21.6 us
    all_to_all x1, blocking collectives, exchange(): return lax.all_to_all(x, 'tensor', split_axis=0, concat_axis=0, tiled=True)  18 us
    all_to_all x1, waiting for transfers between devices, exchange(): return lax.all_to_all(x, 'tensor', split_axis=0, concat_axis=0, tiled=True)  14 us
    pallas_call x1, Pallas kernels, project_queries_keys(): pl.pallas_call(query_key_kernel, in_specs=[pl.BlockSpec(memory_space=SMEM...  6.14 us
    ppermute x7, waiting for transfers between devices, flip(): return lax.ppermute(x, 'context', [(i, i ^ bit) for i in range(16)])  5.14 us
    pallas_call x1, Pallas kernels, project_values(): pl.pallas_call(value_kernel, in_specs=[pl.BlockSpec(memory_space=HBM)] *...  5.07 us
    pallas_call x1, Pallas kernels, attention_weights(): pl.pallas_call(weight_kernel, in_specs=[pl.BlockSpec(memory_space=SMEM)]...  4.56 us
  transfers between devices with their start and end apart: 9, of which 4 were waited for; matrix products, arithmetic and copies ran while one was open for 0% of the time, Pallas kernels for 11%

profile of v3, /device:TPU:1, one launch (start us, length us, event | category | flops | bytes accessed | tf_op | source)
XLA Modules:
  0.0 110.3 jit_solution(17542595919965990223)
XLA Ops:
  0.0 0.0 copy-start.3
  0.0 0.0 copy-start.4
  0.0 0.0 copy-start
  0.0 5.1 %project_values.1 = bf16[384,128]{1,0:T(8,128)(2,1)} custom-call(bf16[384,8192]{1,0:T(8,128)(2,1)} %x_ref.2, bf16[8192,128]{1,0:T(8,128)(2,1)} %w_ref.1), custom_call_target="tpu_custom_call" | custom-call | tf_op jit(solution)/shard_map/project_values/pallas_call | solution.py:73
  5.1 21.6 %all-to-all-start = ((bf16[48,8,128]{2,1,0:T(8,128)(2,1)}), bf16[48,8,128]{2,1,0:T(8,128)(2,1)S(1)}, u32[]{:S(2)}, u32[]{:S(2)}) async-start(bf16[48,8,128]{2,1,0:T(8,128)(2,1)} %bitcast), calls=%async_computation | async-start | bytes 196608 | tf_op jit(solution)/shard_map/all_to_all | solution.py:328
  26.7 0.0 copy-done.3
  26.7 0.1 copy.10
  26.8 0.0 copy-done.4
  26.8 0.1 copy.9
  27.0 14.0 %all-to-all-done.u_ref = bf16[48,8,128]{2,1,0:T(8,128)(2,1)S(1)} async-done(((bf16[48,8,128]{2,1,0:T(8,128)(2,1)}), bf16[48,8,128]{2,1,0:T(8,128)(2,1)S(1)}, u32[]{:S(2)}, u32[]{:S(2)}) %all-to-all-start) | async-done | bytes 98336 | tf_op jit(solution)/shard_map/all_to_all | solution.py:328
  41.0 0.0 copy-done
  41.0 0.5 mix_heads.1
  41.5 18.0 %all_to_all.15 = bf16[48,8,128]{2,1,0:T(8,128)(2,1)S(1)} all-to-all(bf16[48,8,128]{2,1,0:T(8,128)(2,1)S(1)} %mix_heads.1), channel_id=1, replica_groups=mesh['tensor'=48,'context'=16] {'tensor'}, dimensions={0} | all-to-all | bytes 196608 | tf_op jit(solution)/shard_map/all_to_all | solution.py:328
  59.6 1.0 repeat.1
  60.5 4.2 %all-to-all-start.2 = ((bf16[8,384,128]{2,1,0:T(8,128)(2,1)}), bf16[8,384,128]{2,1,0:T(8,128)(2,1)S(1)}, u32[]{:S(2)}, u32[]{:S(2)}) async-start(bf16[8,384,128]{2,1,0:T(8,128)(2,1)} %repeat.1), calls=%async_computation.2 | async-start | bytes 1572864 | tf_op jit(solution)/shard_map/all_to_all | solution.py:331
  64.7 6.1 %project_queries_keys.1 = (bf16[384,128]{1,0:T(8,128)(2,1)}, bf16[1,400,128]{2,1,0:T(8,128)(2,1)S(1)}) custom-call(s32[4]{0:T(128)} %ids_ref.3, bf16[384,8192]{1,0:T(8,128)(2,1)} %x_ref.2, bf16[8192,128]{1,0:T(8,128)(2,1)} %wq_ref.1, bf16[8192,128]{1,0:T(8,128)(2,1)} %wk_ref.1), custom_call_target="tpu_custom_call" | custom-call | tf_op jit(solution)/shard_map/project_queries_keys/pallas_call | solution.py:103
  70.9 4.9 %collective-permute-start.1 = (bf16[1,400,128]{2,1,0:T(8,128)(2,1)S(1)}, bf16[1,400,128]{2,1,0:T(8,128)(2,1)S(1)}, u32[]{:S(2)}, u32[]{:S(2)}) collective-permute-start(bf16[1,400,128]{2,1,0:T(8,128)(2,1)S(1)} %get-tuple-element.14.refs_0_), channel_id=1, source_target_pairs={{0,8},{1,9},{2,10},{3,11},{4,12},{5,13},{6,14},{7,15},{8,0},{9,1},... | collective-permute-start | bytes 307208 | tf_op jit(solution)/shard_map/ppermute | solution.py:336
  75.7 3.1 %collective-permute-start = (bf16[1,400,128]{2,1,0:T(8,128)(2,1)S(1)}, bf16[1,400,128]{2,1,0:T(8,128)(2,1)S(1)}, u32[]{:S(2)}, u32[]{:S(2)}) collective-permute-start(bf16[1,400,128]{2,1,0:T(8,128)(2,1)S(1)} %get-tuple-element.14.refs_0_), channel_id=1, source_target_pairs={{0,2},{1,3},{2,0},{3,1},{4,6},{5,7},{6,4},{7,5},{8,10},{9,11},{10,... | collective-permute-start | bytes 307208 | tf_op jit(solution)/shard_map/ppermute | solution.py:336
  78.8 0.5 collective-permute-done.1.refs_2_
  79.4 2.1 %collective-permute-start.2 = (bf16[1,400,128]{2,1,0:T(8,128)(2,1)S(1)}, bf16[1,400,128]{2,1,0:T(8,128)(2,1)S(1)}, u32[]{:S(2)}, u32[]{:S(2)}) collective-permute-start(bf16[1,400,128]{2,1,0:T(8,128)(2,1)S(1)} %collective-permute-done.1.refs_2_), channel_id=1, source_target_pairs={{0,2},{1,3},{2,0},{3,1},{4,6},{5,7},{6,4},{7,5},{8,10},{9,11},{10,... | collective-permute-start | bytes 307208 | tf_op jit(solution)/shard_map/ppermute | solution.py:336
  81.5 0.0 collective-permute-done.refs_1_
  81.5 3.3 %collective-permute-done.2.refs_3_ = bf16[1,400,128]{2,1,0:T(8,128)(2,1)S(1)} collective-permute-done((bf16[1,400,128]{2,1,0:T(8,128)(2,1)S(1)}, bf16[1,400,128]{2,1,0:T(8,128)(2,1)S(1)}, u32[]{:S(2)}, u32[]{:S(2)}) %collective-permute-start.2) | collective-permute-done | bytes 102432 | tf_op jit(solution)/shard_map/ppermute | solution.py:336
  84.8 1.9 %collective-permute-start.3 = (bf16[4,400,128]{2,1,0:T(8,128)(2,1)S(1)}, bf16[4,400,128]{2,1,0:T(8,128)(2,1)S(1)}, u32[]{:S(2)}, u32[]{:S(2)}) collective-permute-start(bf16[4,400,128]{2,1,0:T(8,128)(2,1)S(1)} %pack.1.refs_0_), channel_id=1, source_target_pairs={{0,4},{1,5},{2,6},{3,7},{4,0},{5,1},{6,2},{7,3},{8,12},{9,13},{10,... | collective-permute-start | bytes 1228808 | tf_op jit(solution)/shard_map/ppermute | solution.py:336
  86.7 0.0 all-to-all-done.2.v_ref
  86.7 8.4 %collective-permute-start.6 = (bf16[8,384,128]{2,1,0:T(8,128)(2,1)S(1)}, bf16[8,384,128]{2,1,0:T(8,128)(2,1)S(1)}, u32[]{:S(2)}, u32[]{:S(2)}) collective-permute-start(bf16[8,384,128]{2,1,0:T(8,128)(2,1)S(1)} %all-to-all-done.2.v_ref), channel_id=1, source_target_pairs={{0,1},{1,0},{2,3},{3,2},{4,5},{5,4},{6,7},{7,6},{8,9},{9,8},{10,11... | collective-permute-start | bytes 2359304 | tf_op jit(solution)/shard_map/ppermute | solution.py:336
  95.2 1.9 %collective-permute-start.4 = (bf16[4,400,128]{2,1,0:T(8,128)(2,1)S(1)}, bf16[4,400,128]{2,1,0:T(8,128)(2,1)S(1)}, u32[]{:S(2)}, u32[]{:S(2)}) collective-permute-start(bf16[4,400,128]{2,1,0:T(8,128)(2,1)S(1)} %pack.1.refs_0_), channel_id=1, source_target_pairs={{0,1},{1,0},{2,3},{3,2},{4,5},{5,4},{6,7},{7,6},{8,9},{9,8},{10,11... | collective-permute-start | bytes 1228808 | tf_op jit(solution)/shard_map/ppermute | solution.py:336
  97.1 0.0 collective-permute-done.3.refs_1_
  97.1 0.0 copy-start.1
  97.1 4.7 %collective-permute-start.5 = (bf16[4,400,128]{2,1,0:T(8,128)(2,1)S(1)}, bf16[4,400,128]{2,1,0:T(8,128)(2,1)S(1)}, u32[]{:S(2)}, u32[]{:S(2)}) collective-permute-start(bf16[4,400,128]{2,1,0:T(8,128)(2,1)S(1)} %collective-permute-done.3.refs_1_), channel_id=1, source_target_pairs={{0,1},{1,0},{2,3},{3,2},{4,5},{5,4},{6,7},{7,6},{8,9},{9,8},{10,11... | collective-permute-start | bytes 1228808 | tf_op jit(solution)/shard_map/ppermute | solution.py:336
  101.9 0.0 collective-permute-done.4.refs_2_
  101.9 0.0 copy-start.2
  101.9 1.3 %collective-permute-done.5.refs_3_ = bf16[4,400,128]{2,1,0:T(8,128)(2,1)S(1)} collective-permute-done((bf16[4,400,128]{2,1,0:T(8,128)(2,1)S(1)}, bf16[4,400,128]{2,1,0:T(8,128)(2,1)S(1)}, u32[]{:S(2)}, u32[]{:S(2)}) %collective-permute-start.5) | collective-permute-done | bytes 409632 | tf_op jit(solution)/shard_map/ppermute | solution.py:336
  103.2 0.0 copy-done.1
  103.2 0.0 copy-done.2
  103.2 4.6 %attention_weights.1 = (bf16[2,192,3072]{2,1,0:T(8,128)(2,1)S(1)}, f32[384,128]{1,0:T(8,128)}) custom-call(s32[4]{0:T(128)} %ids_ref.3, bf16[384,128]{1,0:T(8,128)(2,1)} %get-tuple-element.13.q_ref, bf16[4,400,128]{2,1,0:T(8,128)(2,1)S(1)} %pack.1.refs_0_, bf16[4,400,128]{2,1,0:T(8,128)(2,1)} %copy-done.1, bf16[4,400,128]{2,1,0:T(8,128)(2,1)} %copy-done.2, ...), custom_call_target="tpu_custom_call" | custom-call | tf_op jit(solution)/shard_map/attention_weights/pallas_call | solution.py:210
  107.8 1.4 %apply_first.1 = (f32[384,128]{1,0:T(8,128)S(1)}, f32[384,128]{1,0:T(8,128)S(1)}) custom-call(bf16[2,192,3072]{2,1,0:T(8,128)(2,1)S(1)} %get-tuple-element.15.w_ref, f32[384,128]{1,0:T(8,128)} %get-tuple-element.16.total_ref, bf16[8,384,128]{2,1,0:T(8,128)(2,1)S(1)} %all-to-all-done.2.v_ref), custom_call_target="tpu_custom_call" | custom-call | tf_op jit(solution)/shard_map/apply_first/pallas_call | solution.py:263
  109.2 0.0 collective-permute-done.6.v_ref
  109.2 1.1 %apply_last.1 = bf16[384,128]{1,0:T(8,128)(2,1)} custom-call(bf16[2,192,3072]{2,1,0:T(8,128)(2,1)S(1)} %get-tuple-element.15.w_ref, f32[384,128]{1,0:T(8,128)S(1)} %get-tuple-element.17.total_ref, f32[384,128]{1,0:T(8,128)S(1)} %get-tuple-element.18.part_ref, bf16[8,384,128]{2,1,0:T(8,128)(2,1)S(1)} %collective-permute-done.6.v_ref), custom_call_target="tpu_custom_call" | custom-call | tf_op jit(solution)/shard_map/apply_last/pallas_call | solution.py:274
  (2 shorter events, 0.1 us)
Async XLA Ops:
  0.0 26.7 %copy-start.3 = (bf16[48,96]{1,0:T(8,128)(2,1)S(1)}, bf16[48,96]{1,0:T(8,128)(2,1)}, u32[]{:S(2)}) copy-start(bf16[48,96]{1,0:T(8,128)(2,1)} %param.13) | copy-start | bytes 27652
  0.0 26.8 %copy-start.4 = (bf16[48,96]{1,0:T(8,128)(2,1)S(1)}, bf16[48,96]{1,0:T(8,128)(2,1)}, u32[]{:S(2)}) copy-start(bf16[48,96]{1,0:T(8,128)(2,1)} %param.12) | copy-start | bytes 27652
  0.0 41.0 %copy-start = (bf16[96,48]{0,1:T(8,128)(2,1)S(1)}, bf16[96,48]{0,1:T(8,128)(2,1)}, u32[]{:S(2)}) copy-start(bf16[96,48]{0,1:T(8,128)(2,1)} %param.14) | copy-start | bytes 27652
  5.1 35.9 %all-to-all-start = ((bf16[48,8,128]{2,1,0:T(8,128)(2,1)}), bf16[48,8,128]{2,1,0:T(8,128)(2,1)S(1)}, u32[]{:S(2)}, u32[]{:S(2)}) async-start(bf16[48,8,128]{2,1,0:T(8,128)(2,1)} %bitcast), calls=%async_computation | async-start | bytes 196608 | tf_op jit(solution)/shard_map/all_to_all | solution.py:328
  60.5 26.2 %all-to-all-start.2 = ((bf16[8,384,128]{2,1,0:T(8,128)(2,1)}), bf16[8,384,128]{2,1,0:T(8,128)(2,1)S(1)}, u32[]{:S(2)}, u32[]{:S(2)}) async-start(bf16[8,384,128]{2,1,0:T(8,128)(2,1)} %repeat.1), calls=%async_computation.2 | async-start | bytes 1572864 | tf_op jit(solution)/shard_map/all_to_all | solution.py:331
  70.9 8.5 %collective-permute-start.1 = (bf16[1,400,128]{2,1,0:T(8,128)(2,1)S(1)}, bf16[1,400,128]{2,1,0:T(8,128)(2,1)S(1)}, u32[]{:S(2)}, u32[]{:S(2)}) collective-permute-start(bf16[1,400,128]{2,1,0:T(8,128)(2,1)S(1)} %get-tuple-element.14.refs_0_), channel_id=1, source_target_pairs={{0,8},{1,9},{2,10},{3,11},{4,12},{5,13},{6,14},{7,15},{8,0},{9,1},... | collective-permute-start | bytes 307208 | tf_op jit(solution)/shard_map/ppermute | solution.py:336
  75.7 5.8 %collective-permute-start = (bf16[1,400,128]{2,1,0:T(8,128)(2,1)S(1)}, bf16[1,400,128]{2,1,0:T(8,128)(2,1)S(1)}, u32[]{:S(2)}, u32[]{:S(2)}) collective-permute-start(bf16[1,400,128]{2,1,0:T(8,128)(2,1)S(1)} %get-tuple-element.14.refs_0_), channel_id=1, source_target_pairs={{0,2},{1,3},{2,0},{3,1},{4,6},{5,7},{6,4},{7,5},{8,10},{9,11},{10,... | collective-permute-start | bytes 307208 | tf_op jit(solution)/shard_map/ppermute | solution.py:336
  79.4 5.4 %collective-permute-start.2 = (bf16[1,400,128]{2,1,0:T(8,128)(2,1)S(1)}, bf16[1,400,128]{2,1,0:T(8,128)(2,1)S(1)}, u32[]{:S(2)}, u32[]{:S(2)}) collective-permute-start(bf16[1,400,128]{2,1,0:T(8,128)(2,1)S(1)} %collective-permute-done.1.refs_2_), channel_id=1, source_target_pairs={{0,2},{1,3},{2,0},{3,1},{4,6},{5,7},{6,4},{7,5},{8,10},{9,11},{10,... | collective-permute-start | bytes 307208 | tf_op jit(solution)/shard_map/ppermute | solution.py:336
  84.8 12.3 %collective-permute-start.3 = (bf16[4,400,128]{2,1,0:T(8,128)(2,1)S(1)}, bf16[4,400,128]{2,1,0:T(8,128)(2,1)S(1)}, u32[]{:S(2)}, u32[]{:S(2)}) collective-permute-start(bf16[4,400,128]{2,1,0:T(8,128)(2,1)S(1)} %pack.1.refs_0_), channel_id=1, source_target_pairs={{0,4},{1,5},{2,6},{3,7},{4,0},{5,1},{6,2},{7,3},{8,12},{9,13},{10,... | collective-permute-start | bytes 1228808 | tf_op jit(solution)/shard_map/ppermute | solution.py:336
  86.7 22.4 %collective-permute-start.6 = (bf16[8,384,128]{2,1,0:T(8,128)(2,1)S(1)}, bf16[8,384,128]{2,1,0:T(8,128)(2,1)S(1)}, u32[]{:S(2)}, u32[]{:S(2)}) collective-permute-start(bf16[8,384,128]{2,1,0:T(8,128)(2,1)S(1)} %all-to-all-done.2.v_ref), channel_id=1, source_target_pairs={{0,1},{1,0},{2,3},{3,2},{4,5},{5,4},{6,7},{7,6},{8,9},{9,8},{10,11... | collective-permute-start | bytes 2359304 | tf_op jit(solution)/shard_map/ppermute | solution.py:336
  95.2 6.7 %collective-permute-start.4 = (bf16[4,400,128]{2,1,0:T(8,128)(2,1)S(1)}, bf16[4,400,128]{2,1,0:T(8,128)(2,1)S(1)}, u32[]{:S(2)}, u32[]{:S(2)}) collective-permute-start(bf16[4,400,128]{2,1,0:T(8,128)(2,1)S(1)} %pack.1.refs_0_), channel_id=1, source_target_pairs={{0,1},{1,0},{2,3},{3,2},{4,5},{5,4},{6,7},{7,6},{8,9},{9,8},{10,11... | collective-permute-start | bytes 1228808 | tf_op jit(solution)/shard_map/ppermute | solution.py:336
  97.1 6.1 %copy-start.1 = (bf16[4,400,128]{2,1,0:T(8,128)(2,1)}, bf16[4,400,128]{2,1,0:T(8,128)(2,1)S(1)}, u32[]{:S(2)}) copy-start(bf16[4,400,128]{2,1,0:T(8,128)(2,1)S(1)} %collective-permute-done.3.refs_1_) | copy-start | bytes 1228804
  97.1 6.1 %collective-permute-start.5 = (bf16[4,400,128]{2,1,0:T(8,128)(2,1)S(1)}, bf16[4,400,128]{2,1,0:T(8,128)(2,1)S(1)}, u32[]{:S(2)}, u32[]{:S(2)}) collective-permute-start(bf16[4,400,128]{2,1,0:T(8,128)(2,1)S(1)} %collective-permute-done.3.refs_1_), channel_id=1, source_target_pairs={{0,1},{1,0},{2,3},{3,2},{4,5},{5,4},{6,7},{7,6},{8,9},{9,8},{10,11... | collective-permute-start | bytes 1228808 | tf_op jit(solution)/shard_map/ppermute | solution.py:336
  101.9 1.3 %copy-start.2 = (bf16[4,400,128]{2,1,0:T(8,128)(2,1)}, bf16[4,400,128]{2,1,0:T(8,128)(2,1)S(1)}, u32[]{:S(2)}) copy-start(bf16[4,400,128]{2,1,0:T(8,128)(2,1)S(1)} %collective-permute-done.4.refs_2_) | copy-start | bytes 1228804

commit v4 on v3

--- a/solution.py
+++ b/solution.py
@@ -10,6 +10,7 @@
 BLK = 96
 PAD = 16
 CHUNKS = 8
+STEPS = (0, 3, 1, 2)
 CORE_GROUPS = [[2 * k + core for k in range(8)] for core in range(2)]
 VMEM = pltpu.MemorySpace.VMEM
 SMEM = pltpu.MemorySpace.SMEM
@@ -145,14 +146,7 @@
 
 
 def weight_kernel(ids_ref, q_ref, *refs):
-    quad_ref, near_ref, far_quad_ref, far_near_ref, w_ref, total_ref, s_ref, *held, sems = refs
-    copies = [
-        pltpu.make_async_copy(ref, keep, sems.at[n])
-        for n, (ref, keep) in enumerate(zip((near_ref, far_quad_ref), held))
-    ]
-    for copy in copies:
-        copy.start()
-    key_refs = [quad_ref, *held, far_near_ref]
+    *key_refs, w_ref, total_ref, s_ref = refs
     half = q_ref.shape[0] // 2
     rows = q_ref.shape[0]
     chunk = 2 * half
@@ -170,8 +164,6 @@
         at = 0
         for first in range(0, len(sources), 2):
             pair = sources[first : first + 2]
-            if s == 0 and first in (4, 8):
-                copies[first // 4 - 1].wait()
             keys = jnp.concatenate(
                 [k_ref[d, s * half : (s + 1) * half, :] for k_ref, d in pair], axis=0
             )
@@ -206,25 +198,19 @@
     rows = queries.shape[0]
     half = rows // 2
     count = sum(piece.shape[0] for piece in keys) * half
-    places = [on_chip, off_chip, off_chip, on_chip]
     return pl.pallas_call(
         weight_kernel,
         in_specs=[pl.BlockSpec(memory_space=SMEM)]
-        + [pl.BlockSpec(memory_space=space) for space in (VMEM, VMEM, HBM, HBM, VMEM)],
+        + [pl.BlockSpec(memory_space=VMEM)] * (1 + len(keys)),
         out_specs=[pl.BlockSpec(memory_space=VMEM)] * 2,
         out_shape=[
             in_vmem((2, half, count), jnp.bfloat16),
             pltpu.HBM((rows, HEAD_DIM), jnp.float32),
         ],
-        scratch_shapes=[
-            pltpu.VMEM((half, count), jnp.float32),
-            pltpu.VMEM(keys[1].shape, jnp.bfloat16),
-            pltpu.VMEM(keys[2].shape, jnp.bfloat16),
-            pltpu.SemaphoreType.DMA((2,)),
-        ],
+        scratch_shapes=[pltpu.VMEM((half, count), jnp.float32)],
         compiler_params=GRANT,
         name="attention_weights",
-    )(off_chip(block_ids), off_chip(queries), *[place(k) for place, k in zip(places, keys)])
+    )(off_chip(block_ids), off_chip(queries), *[on_chip(k) for k in keys])
 
 
 def summed(w_ref, v_ref, s, first):
@@ -233,9 +219,9 @@
     mine = lax.axis_index("context") // 2
     acc = jnp.zeros((half, HEAD_DIM), jnp.float32)
     for d in range(0, v_ref.shape[0], sources):
-        turns = [e % 2 + e // 2 % 2 * 4 + e // 4 * 2 for e in range(d, d + sources)]
+        spots = [((mine + 2 * STEPS[e // 2]) & 7) ^ (e % 2) for e in range(d, d + sources)]
         values = jnp.concatenate(
-            [v_ref[mine ^ turn, s * half : (s + 1) * half, :] for turn in turns], axis=0
+            [v_ref[spot, s * half : (s + 1) * half, :] for spot in spots], axis=0
         )
         at = first + d * half
         acc = acc + jnp.dot(
@@ -283,16 +269,19 @@
 
 def pack_kernel(*refs):
     *pieces, out_ref = refs
-    for n, piece in enumerate(pieces):
-        out_ref[n] = piece[0]
+    n = 0
+    for piece in pieces:
+        out_ref[n : n + piece.shape[0]] = piece[...]
+        n += piece.shape[0]
 
 
 def pack(*pieces):
+    count = sum(piece.shape[0] for piece in pieces)
     return pl.pallas_call(
         pack_kernel,
         in_specs=[pl.BlockSpec(memory_space=VMEM)] * len(pieces),
         out_specs=pl.BlockSpec(memory_space=VMEM),
-        out_shape=in_vmem((len(pieces), *pieces[0].shape[1:]), pieces[0].dtype),
+        out_shape=in_vmem((count, *pieces[0].shape[1:]), pieces[0].dtype),
         compiler_params=GRANT,
         name="pack",
     )(*[on_chip(piece) for piece in pieces])
@@ -335,6 +324,9 @@
     def flip(x, bit):
         return lax.ppermute(x, "context", [(i, i ^ bit) for i in range(16)])
 
+    def along(x, step):
+        return lax.ppermute(x, "context", [(i, (i + 4 * step) % 16) for i in range(16)])
+
     w_in = jnp.concatenate([mix_gate, mix_up], axis=1).T
     w_out = mix_down.T
     values = project_values(tokens, w_value)
@@ -342,16 +334,15 @@
     tokens, values = lax.optimization_barrier((tokens, values))
     queries, own = project_queries_keys(block_ids, tokens, w_query, w_key)
     beside = flip(own, 2)
-    far = flip(own, 8)
     mixed = mix(gathered, w_in, w_out)
     mixed_rows = exchange(mixed).reshape(rows, HEAD_DIM)
-    far_beside = flip(far, 2)
-    quad = pack(own, beside, far, far_beside)
-    near = flip(quad, 4)
-    other_quad = flip(quad, 1)
-    other_near = flip(near, 1)
-    keys = [quad, near, other_quad, other_near]
-    weights, total = attention_weights(block_ids, queries, keys)
+    pair = pack(own, beside)
+    up = along(pair, 1)
+    down = along(pair, 3)
+    far = along(pair, 2)
+    keys = pack(pair, up, down, far)
+    other_keys = flip(keys, 1)
+    weights, total = attention_weights(block_ids, queries, [keys, other_keys])
     copies = repeat(mixed_rows, 8)
     values_mine = spread(copies)
     values_other = flip(values_mine, 1)

time: 111 us -> 108 us (0.973)
  starting transfers between devices: 52.9 us -> 47 us
  waiting for transfers between devices: 19.1 us -> 23.2 us
    ppermute x7 -> x3, starting transfers between devices: 27.1 us -> 11.6 us  [flip(): return lax.ppermute(x, 'context', [(i, i ^ bit) for i in range(16)])]
    ppermute x0 -> x3, starting transfers between devices: none -> 9.58 us  [along(): lax.ppermute(x, 'context', [(i, (i + 4 * step) % 16) for i in range(16)])]
    ppermute x0 -> x3, waiting for transfers between devices: none -> 6.04 us  [along(): lax.ppermute(x, 'context', [(i, (i + 4 * step) % 16) for i in range(16)])]
    ppermute x7 -> x3, waiting for transfers between devices: 5.14 us -> 3.18 us  [flip(): return lax.ppermute(x, 'context', [(i, i ^ bit) for i in range(16)])]
  transfers between devices with their start and end apart: 9 -> 8, of which waited for: 4 -> 3; matrix products, arithmetic and copies ran while one was open for 0% -> 0% of each run, Pallas kernels for 11% -> 10%
where the time goes in v4:
time: 108 us
  starting transfers between devices  47 us (44%)
  waiting for transfers between devices  23.2 us (21%)
  Pallas kernels  18.8 us (17%)
  blocking collectives  18 us (17%)
    all_to_all x1, starting transfers between devices, exchange(): return lax.all_to_all(x, 'tensor', split_axis=0, concat_axis=0, tiled=True)  21.6 us
    all_to_all x1, blocking collectives, exchange(): return lax.all_to_all(x, 'tensor', split_axis=0, concat_axis=0, tiled=True)  18 us
    all_to_all x1, waiting for transfers between devices, exchange(): return lax.all_to_all(x, 'tensor', split_axis=0, concat_axis=0, tiled=True)  14 us
    ppermute x3, starting transfers between devices, flip(): return lax.ppermute(x, 'context', [(i, i ^ bit) for i in range(16)])  11.6 us
    ppermute x3, starting transfers between devices, along(): lax.ppermute(x, 'context', [(i, (i + 4 * step) % 16) for i in range(16)])  9.58 us
    pallas_call x1, Pallas kernels, project_queries_keys(): pl.pallas_call(query_key_kernel, in_specs=[pl.BlockSpec(memory_space=SMEM...  6.15 us
    ppermute x3, waiting for transfers between devices, along(): lax.ppermute(x, 'context', [(i, (i + 4 * step) % 16) for i in range(16)])  6.04 us
    pallas_call x1, Pallas kernels, project_values(): pl.pallas_call(value_kernel, in_specs=[pl.BlockSpec(memory_space=HBM)] *...  5.07 us
  transfers between devices with their start and end apart: 8, of which 3 were waited for; matrix products, arithmetic and copies ran while one was open for 0% of the time, Pallas kernels for 10%

profile of v4, /device:TPU:1, one launch (start us, length us, event | category | flops | bytes accessed | tf_op | source)
XLA Modules:
  0.0 107.5 jit_solution(11810108072434158506)
XLA Ops:
  0.0 0.0 copy-start.1
  0.0 0.0 copy-start.2
  0.0 0.0 copy-start
  0.0 5.1 %project_values.1 = bf16[384,128]{1,0:T(8,128)(2,1)} custom-call(bf16[384,8192]{1,0:T(8,128)(2,1)} %x_ref.2, bf16[8192,128]{1,0:T(8,128)(2,1)} %w_ref.1), custom_call_target="tpu_custom_call" | custom-call | tf_op jit(solution)/shard_map/project_values/pallas_call | solution.py:74
  5.1 21.6 %all-to-all-start = ((bf16[48,8,128]{2,1,0:T(8,128)(2,1)}), bf16[48,8,128]{2,1,0:T(8,128)(2,1)S(1)}, u32[]{:S(2)}, u32[]{:S(2)}) async-start(bf16[48,8,128]{2,1,0:T(8,128)(2,1)} %bitcast), calls=%async_computation | async-start | bytes 196608 | tf_op jit(solution)/shard_map/all_to_all | solution.py:317
  26.7 0.0 copy-done.1
  26.7 0.1 copy.10
  26.8 0.0 copy-done.2
  26.8 0.1 copy.9
  27.0 14.0 %all-to-all-done.u_ref = bf16[48,8,128]{2,1,0:T(8,128)(2,1)S(1)} async-done(((bf16[48,8,128]{2,1,0:T(8,128)(2,1)}), bf16[48,8,128]{2,1,0:T(8,128)(2,1)S(1)}, u32[]{:S(2)}, u32[]{:S(2)}) %all-to-all-start) | async-done | bytes 98336 | tf_op jit(solution)/shard_map/all_to_all | solution.py:317
  41.0 0.0 copy-done
  41.0 0.5 mix_heads.1
  41.5 18.0 %all_to_all.15 = bf16[48,8,128]{2,1,0:T(8,128)(2,1)S(1)} all-to-all(bf16[48,8,128]{2,1,0:T(8,128)(2,1)S(1)} %mix_heads.1), channel_id=1, replica_groups=mesh['tensor'=48,'context'=16] {'tensor'}, dimensions={0} | all-to-all | bytes 196608 | tf_op jit(solution)/shard_map/all_to_all | solution.py:317
  59.6 1.0 repeat.1
  60.5 4.2 %all-to-all-start.2 = ((bf16[8,384,128]{2,1,0:T(8,128)(2,1)}), bf16[8,384,128]{2,1,0:T(8,128)(2,1)S(1)}, u32[]{:S(2)}, u32[]{:S(2)}) async-start(bf16[8,384,128]{2,1,0:T(8,128)(2,1)} %repeat.1), calls=%async_computation.2 | async-start | bytes 1572864 | tf_op jit(solution)/shard_map/all_to_all | solution.py:320
  64.7 6.1 %project_queries_keys.1 = (bf16[384,128]{1,0:T(8,128)(2,1)}, bf16[1,400,128]{2,1,0:T(8,128)(2,1)S(1)}) custom-call(s32[4]{0:T(128)} %ids_ref.3, bf16[384,8192]{1,0:T(8,128)(2,1)} %x_ref.2, bf16[8192,128]{1,0:T(8,128)(2,1)} %wq_ref.1, bf16[8192,128]{1,0:T(8,128)(2,1)} %wk_ref.1), custom_call_target="tpu_custom_call" | custom-call | tf_op jit(solution)/shard_map/project_queries_keys/pallas_call | solution.py:104
  70.9 3.4 %collective-permute-start = (bf16[1,400,128]{2,1,0:T(8,128)(2,1)S(1)}, bf16[1,400,128]{2,1,0:T(8,128)(2,1)S(1)}, u32[]{:S(2)}, u32[]{:S(2)}) collective-permute-start(bf16[1,400,128]{2,1,0:T(8,128)(2,1)S(1)} %get-tuple-element.14.refs_0_), channel_id=1, source_target_pairs={{0,2},{1,3},{2,0},{3,1},{4,6},{5,7},{6,4},{7,5},{8,10},{9,11},{10,... | collective-permute-start | bytes 307208 | tf_op jit(solution)/shard_map/ppermute | solution.py:325
  74.2 3.2 %collective-permute-done.refs_1_ = bf16[1,400,128]{2,1,0:T(8,128)(2,1)S(1)} collective-permute-done((bf16[1,400,128]{2,1,0:T(8,128)(2,1)S(1)}, bf16[1,400,128]{2,1,0:T(8,128)(2,1)S(1)}, u32[]{:S(2)}, u32[]{:S(2)}) %collective-permute-start) | collective-permute-done | bytes 102432 | tf_op jit(solution)/shard_map/ppermute | solution.py:325
  77.4 2.8 %collective-permute-start.1 = (bf16[2,400,128]{2,1,0:T(8,128)(2,1)S(1)}, bf16[2,400,128]{2,1,0:T(8,128)(2,1)S(1)}, u32[]{:S(2)}, u32[]{:S(2)}) collective-permute-start(bf16[2,400,128]{2,1,0:T(8,128)(2,1)S(1)} %pack.2.refs_0_), channel_id=1, source_target_pairs={{0,4},{1,5},{2,6},{3,7},{4,8},{5,9},{6,10},{7,11},{8,12},{9,13},{1... | collective-permute-start | bytes 614408 | tf_op jit(solution)/shard_map/ppermute | solution.py:328
  80.3 3.7 %collective-permute-start.2 = (bf16[2,400,128]{2,1,0:T(8,128)(2,1)S(1)}, bf16[2,400,128]{2,1,0:T(8,128)(2,1)S(1)}, u32[]{:S(2)}, u32[]{:S(2)}) collective-permute-start(bf16[2,400,128]{2,1,0:T(8,128)(2,1)S(1)} %pack.2.refs_0_), channel_id=1, source_target_pairs={{0,12},{1,13},{2,14},{3,15},{4,0},{5,1},{6,2},{7,3},{8,4},{9,5},{1... | collective-permute-start | bytes 614408 | tf_op jit(solution)/shard_map/ppermute | solution.py:328
  84.0 3.1 %collective-permute-start.3 = (bf16[2,400,128]{2,1,0:T(8,128)(2,1)S(1)}, bf16[2,400,128]{2,1,0:T(8,128)(2,1)S(1)}, u32[]{:S(2)}, u32[]{:S(2)}) collective-permute-start(bf16[2,400,128]{2,1,0:T(8,128)(2,1)S(1)} %pack.2.refs_0_), channel_id=1, source_target_pairs={{0,8},{1,9},{2,10},{3,11},{4,12},{5,13},{6,14},{7,15},{8,0},{9,1},... | collective-permute-start | bytes 614408 | tf_op jit(solution)/shard_map/ppermute | solution.py:328
  87.0 0.0 collective-permute-done.1.refs_1_
  87.1 0.0 collective-permute-done.2.refs_2_
  87.1 6.0 %collective-permute-done.3.refs_3_ = bf16[2,400,128]{2,1,0:T(8,128)(2,1)S(1)} collective-permute-done((bf16[2,400,128]{2,1,0:T(8,128)(2,1)S(1)}, bf16[2,400,128]{2,1,0:T(8,128)(2,1)S(1)}, u32[]{:S(2)}, u32[]{:S(2)}) %collective-permute-start.3) | collective-permute-done | bytes 204832 | tf_op jit(solution)/shard_map/ppermute | solution.py:328
  93.1 0.1 pack.3.refs_0_
  93.2 6.3 %collective-permute-start.4 = (bf16[8,400,128]{2,1,0:T(8,128)(2,1)S(1)}, bf16[8,400,128]{2,1,0:T(8,128)(2,1)S(1)}, u32[]{:S(2)}, u32[]{:S(2)}) collective-permute-start(bf16[8,400,128]{2,1,0:T(8,128)(2,1)S(1)} %pack.3.refs_0_), channel_id=1, source_target_pairs={{0,1},{1,0},{2,3},{3,2},{4,5},{5,4},{6,7},{7,6},{8,9},{9,8},{10,11... | collective-permute-start | bytes 2457608 | tf_op jit(solution)/shard_map/ppermute | solution.py:325
  99.5 0.0 all-to-all-done.2.v_ref
  99.5 1.9 %collective-permute-start.5 = (bf16[8,384,128]{2,1,0:T(8,128)(2,1)S(1)}, bf16[8,384,128]{2,1,0:T(8,128)(2,1)S(1)}, u32[]{:S(2)}, u32[]{:S(2)}) collective-permute-start(bf16[8,384,128]{2,1,0:T(8,128)(2,1)S(1)} %all-to-all-done.2.v_ref), channel_id=1, source_target_pairs={{0,1},{1,0},{2,3},{3,2},{4,5},{5,4},{6,7},{7,6},{8,9},{9,8},{10,11... | collective-permute-start | bytes 2359304 | tf_op jit(solution)/shard_map/ppermute | solution.py:325
  101.4 0.0 collective-permute-done.4.refs_1_
  101.4 3.5 %attention_weights.1 = (bf16[2,192,3072]{2,1,0:T(8,128)(2,1)S(1)}, f32[384,128]{1,0:T(8,128)}) custom-call(s32[4]{0:T(128)} %ids_ref.3, bf16[384,128]{1,0:T(8,128)(2,1)} %get-tuple-element.13.q_ref, bf16[8,400,128]{2,1,0:T(8,128)(2,1)S(1)} %pack.3.refs_0_, bf16[8,400,128]{2,1,0:T(8,128)(2,1)S(1)} %collective-permute-done.4.refs_1_), custom_call_target="tpu_custom_call" | custom-call | tf_op jit(solution)/shard_map/attention_weights/pallas_call | solution.py:201
  105.0 1.4 %apply_first.1 = (f32[384,128]{1,0:T(8,128)S(1)}, f32[384,128]{1,0:T(8,128)S(1)}) custom-call(bf16[2,192,3072]{2,1,0:T(8,128)(2,1)S(1)} %get-tuple-element.15.w_ref, f32[384,128]{1,0:T(8,128)} %get-tuple-element.16.total_ref, bf16[8,384,128]{2,1,0:T(8,128)(2,1)S(1)} %all-to-all-done.2.v_ref), custom_call_target="tpu_custom_call" | custom-call | tf_op jit(solution)/shard_map/apply_first/pallas_call | solution.py:249
  106.4 0.0 collective-permute-done.5.v_ref
  106.4 1.1 %apply_last.1 = bf16[384,128]{1,0:T(8,128)(2,1)} custom-call(bf16[2,192,3072]{2,1,0:T(8,128)(2,1)S(1)} %get-tuple-element.15.w_ref, f32[384,128]{1,0:T(8,128)S(1)} %get-tuple-element.17.total_ref, f32[384,128]{1,0:T(8,128)S(1)} %get-tuple-element.18.part_ref, bf16[8,384,128]{2,1,0:T(8,128)(2,1)S(1)} %collective-permute-done.5.v_ref), custom_call_target="tpu_custom_call" | custom-call | tf_op jit(solution)/shard_map/apply_last/pallas_call | solution.py:260
  (2 shorter events, 0.0 us)
Async XLA Ops:
  0.0 26.7 %copy-start.1 = (bf16[48,96]{1,0:T(8,128)(2,1)S(1)}, bf16[48,96]{1,0:T(8,128)(2,1)}, u32[]{:S(2)}) copy-start(bf16[48,96]{1,0:T(8,128)(2,1)} %param.13) | copy-start | bytes 27652
  0.0 26.8 %copy-start.2 = (bf16[48,96]{1,0:T(8,128)(2,1)S(1)}, bf16[48,96]{1,0:T(8,128)(2,1)}, u32[]{:S(2)}) copy-start(bf16[48,96]{1,0:T(8,128)(2,1)} %param.12) | copy-start | bytes 27652
  0.0 41.0 %copy-start = (bf16[96,48]{0,1:T(8,128)(2,1)S(1)}, bf16[96,48]{0,1:T(8,128)(2,1)}, u32[]{:S(2)}) copy-start(bf16[96,48]{0,1:T(8,128)(2,1)} %param.14) | copy-start | bytes 27652
  5.1 35.9 %all-to-all-start = ((bf16[48,8,128]{2,1,0:T(8,128)(2,1)}), bf16[48,8,128]{2,1,0:T(8,128)(2,1)S(1)}, u32[]{:S(2)}, u32[]{:S(2)}) async-start(bf16[48,8,128]{2,1,0:T(8,128)(2,1)} %bitcast), calls=%async_computation | async-start | bytes 196608 | tf_op jit(solution)/shard_map/all_to_all | solution.py:317
  60.5 38.9 %all-to-all-start.2 = ((bf16[8,384,128]{2,1,0:T(8,128)(2,1)}), bf16[8,384,128]{2,1,0:T(8,128)(2,1)S(1)}, u32[]{:S(2)}, u32[]{:S(2)}) async-start(bf16[8,384,128]{2,1,0:T(8,128)(2,1)} %repeat.1), calls=%async_computation.2 | async-start | bytes 1572864 | tf_op jit(solution)/shard_map/all_to_all | solution.py:320
  70.9 6.6 %collective-permute-start = (bf16[1,400,128]{2,1,0:T(8,128)(2,1)S(1)}, bf16[1,400,128]{2,1,0:T(8,128)(2,1)S(1)}, u32[]{:S(2)}, u32[]{:S(2)}) collective-permute-start(bf16[1,400,128]{2,1,0:T(8,128)(2,1)S(1)} %get-tuple-element.14.refs_0_), channel_id=1, source_target_pairs={{0,2},{1,3},{2,0},{3,1},{4,6},{5,7},{6,4},{7,5},{8,10},{9,11},{10,... | collective-permute-start | bytes 307208 | tf_op jit(solution)/shard_map/ppermute | solution.py:325
  77.4 9.6 %collective-permute-start.1 = (bf16[2,400,128]{2,1,0:T(8,128)(2,1)S(1)}, bf16[2,400,128]{2,1,0:T(8,128)(2,1)S(1)}, u32[]{:S(2)}, u32[]{:S(2)}) collective-permute-start(bf16[2,400,128]{2,1,0:T(8,128)(2,1)S(1)} %pack.2.refs_0_), channel_id=1, source_target_pairs={{0,4},{1,5},{2,6},{3,7},{4,8},{5,9},{6,10},{7,11},{8,12},{9,13},{1... | collective-permute-start | bytes 614408 | tf_op jit(solution)/shard_map/ppermute | solution.py:328
  80.3 6.8 %collective-permute-start.2 = (bf16[2,400,128]{2,1,0:T(8,128)(2,1)S(1)}, bf16[2,400,128]{2,1,0:T(8,128)(2,1)S(1)}, u32[]{:S(2)}, u32[]{:S(2)}) collective-permute-start(bf16[2,400,128]{2,1,0:T(8,128)(2,1)S(1)} %pack.2.refs_0_), channel_id=1, source_target_pairs={{0,12},{1,13},{2,14},{3,15},{4,0},{5,1},{6,2},{7,3},{8,4},{9,5},{1... | collective-permute-start | bytes 614408 | tf_op jit(solution)/shard_map/ppermute | solution.py:328
  84.0 9.1 %collective-permute-start.3 = (bf16[2,400,128]{2,1,0:T(8,128)(2,1)S(1)}, bf16[2,400,128]{2,1,0:T(8,128)(2,1)S(1)}, u32[]{:S(2)}, u32[]{:S(2)}) collective-permute-start(bf16[2,400,128]{2,1,0:T(8,128)(2,1)S(1)} %pack.2.refs_0_), channel_id=1, source_target_pairs={{0,8},{1,9},{2,10},{3,11},{4,12},{5,13},{6,14},{7,15},{8,0},{9,1},... | collective-permute-start | bytes 614408 | tf_op jit(solution)/shard_map/ppermute | solution.py:328
  93.2 8.3 %collective-permute-start.4 = (bf16[8,400,128]{2,1,0:T(8,128)(2,1)S(1)}, bf16[8,400,128]{2,1,0:T(8,128)(2,1)S(1)}, u32[]{:S(2)}, u32[]{:S(2)}) collective-permute-start(bf16[8,400,128]{2,1,0:T(8,128)(2,1)S(1)} %pack.3.refs_0_), channel_id=1, source_target_pairs={{0,1},{1,0},{2,3},{3,2},{4,5},{5,4},{6,7},{7,6},{8,9},{9,8},{10,11... | collective-permute-start | bytes 2457608 | tf_op jit(solution)/shard_map/ppermute | solution.py:325
  99.5 6.9 %collective-permute-start.5 = (bf16[8,384,128]{2,1,0:T(8,128)(2,1)S(1)}, bf16[8,384,128]{2,1,0:T(8,128)(2,1)S(1)}, u32[]{:S(2)}, u32[]{:S(2)}) collective-permute-start(bf16[8,384,128]{2,1,0:T(8,128)(2,1)S(1)} %all-to-all-done.2.v_ref), channel_id=1, source_target_pairs={{0,1},{1,0},{2,3},{3,2},{4,5},{5,4},{6,7},{7,6},{8,9},{9,8},{10,11... | collective-permute-start | bytes 2359304 | tf_op jit(solution)/shard_map/ppermute | solution.py:325

commit v5 on v4

--- a/solution.py
+++ b/solution.py
@@ -10,7 +10,7 @@
 BLK = 96
 PAD = 16
 CHUNKS = 8
-STEPS = (0, 3, 1, 2)
+STEPS = (0, 1, 3, 2)
 CORE_GROUPS = [[2 * k + core for k in range(8)] for core in range(2)]
 VMEM = pltpu.MemorySpace.VMEM
 SMEM = pltpu.MemorySpace.SMEM
@@ -219,7 +219,7 @@
     mine = lax.axis_index("context") // 2
     acc = jnp.zeros((half, HEAD_DIM), jnp.float32)
     for d in range(0, v_ref.shape[0], sources):
-        spots = [((mine + 2 * STEPS[e // 2]) & 7) ^ (e % 2) for e in range(d, d + sources)]
+        spots = [mine ^ (2 * STEPS[e // 2] + e % 2) for e in range(d, d + sources)]
         values = jnp.concatenate(
             [v_ref[spot, s * half : (s + 1) * half, :] for spot in spots], axis=0
         )
@@ -323,9 +323,6 @@
 
     def flip(x, bit):
         return lax.ppermute(x, "context", [(i, i ^ bit) for i in range(16)])
-
-    def along(x, step):
-        return lax.ppermute(x, "context", [(i, (i + 4 * step) % 16) for i in range(16)])
 
     w_in = jnp.concatenate([mix_gate, mix_up], axis=1).T
     w_out = mix_down.T
@@ -337,10 +334,10 @@
     mixed = mix(gathered, w_in, w_out)
     mixed_rows = exchange(mixed).reshape(rows, HEAD_DIM)
     pair = pack(own, beside)
-    up = along(pair, 1)
-    down = along(pair, 3)
-    far = along(pair, 2)
-    keys = pack(pair, up, down, far)
+    near = flip(pair, 4)
+    wrap = flip(pair, 12)
+    far = flip(pair, 8)
+    keys = pack(pair, near, wrap, far)
     other_keys = flip(keys, 1)
     weights, total = attention_weights(block_ids, queries, [keys, other_keys])
     copies = repeat(mixed_rows, 8)

time: 108 us -> 109 us (level)
    ppermute x3 -> x6, starting transfers between devices: 11.6 us -> 21.4 us  [flip(): return lax.ppermute(x, 'context', [(i, i ^ bit) for i in range(16)])]
    ppermute x3 -> x0, starting transfers between devices: 9.58 us -> none  [along(): lax.ppermute(x, 'context', [(i, (i + 4 * step) % 16) for i in range(16)])]
    ppermute x3 -> x6, waiting for transfers between devices: 3.18 us -> 9.84 us  [flip(): return lax.ppermute(x, 'context', [(i, i ^ bit) for i in range(16)])]
    ppermute x3 -> x0, waiting for transfers between devices: 6.04 us -> none  [along(): lax.ppermute(x, 'context', [(i, (i + 4 * step) % 16) for i in range(16)])]
  transfers between devices with their start and end apart: 8 -> 8, of which waited for: 3 -> 4; matrix products, arithmetic and copies ran while one was open for 0% -> 0% of each run, Pallas kernels for 10% -> 10%
where the time goes in v5:
time: 109 us; the launch traced here: 108 us
  starting transfers between devices  47.2 us (43%)
  waiting for transfers between devices  23.8 us (22%)
  Pallas kernels  18.8 us (17%)
  blocking collectives  18 us (17%)
    all_to_all x1, starting transfers between devices, exchange(): return lax.all_to_all(x, 'tensor', split_axis=0, concat_axis=0, tiled=True)  21.6 us
    ppermute x6, starting transfers between devices, flip(): return lax.ppermute(x, 'context', [(i, i ^ bit) for i in range(16)])  21.4 us
    all_to_all x1, blocking collectives, exchange(): return lax.all_to_all(x, 'tensor', split_axis=0, concat_axis=0, tiled=True)  18 us
    all_to_all x1, waiting for transfers between devices, exchange(): return lax.all_to_all(x, 'tensor', split_axis=0, concat_axis=0, tiled=True)  14 us
    ppermute x6, waiting for transfers between devices, flip(): return lax.ppermute(x, 'context', [(i, i ^ bit) for i in range(16)])  9.84 us
    pallas_call x1, Pallas kernels, project_queries_keys(): pl.pallas_call(query_key_kernel, in_specs=[pl.BlockSpec(memory_space=SMEM...  6.15 us
    pallas_call x1, Pallas kernels, project_values(): pl.pallas_call(value_kernel, in_specs=[pl.BlockSpec(memory_space=HBM)] *...  5.07 us
    all_to_all x1, starting transfers between devices, spread(): lax.all_to_all(x, 'context', split_axis=0, concat_axis=0, axis_index_grou...  4.18 us
  transfers between devices with their start and end apart: 8, of which 4 were waited for; matrix products, arithmetic and copies ran while one was open for 0% of the time, Pallas kernels for 10%

profile of v5, /device:TPU:1, one launch (start us, length us, event | category | flops | bytes accessed | tf_op | source)
XLA Modules:
  0.0 108.4 jit_solution(7495270011120638501)
XLA Ops:
  0.0 0.0 copy-start.1
  0.0 0.0 copy-start.2
  0.0 0.0 copy-start
  0.0 5.1 %project_values.1 = bf16[384,128]{1,0:T(8,128)(2,1)} custom-call(bf16[384,8192]{1,0:T(8,128)(2,1)} %x_ref.2, bf16[8192,128]{1,0:T(8,128)(2,1)} %w_ref.1), custom_call_target="tpu_custom_call" | custom-call | tf_op jit(solution)/shard_map/project_values/pallas_call | solution.py:74
  5.1 21.6 %all-to-all-start = ((bf16[48,8,128]{2,1,0:T(8,128)(2,1)}), bf16[48,8,128]{2,1,0:T(8,128)(2,1)S(1)}, u32[]{:S(2)}, u32[]{:S(2)}) async-start(bf16[48,8,128]{2,1,0:T(8,128)(2,1)} %bitcast), calls=%async_computation | async-start | bytes 196608 | tf_op jit(solution)/shard_map/all_to_all | solution.py:317
  26.7 0.0 copy-done.1
  26.7 0.1 copy.10
  26.8 0.0 copy-done.2
  26.8 0.1 copy.9
  27.0 14.0 %all-to-all-done.u_ref = bf16[48,8,128]{2,1,0:T(8,128)(2,1)S(1)} async-done(((bf16[48,8,128]{2,1,0:T(8,128)(2,1)}), bf16[48,8,128]{2,1,0:T(8,128)(2,1)S(1)}, u32[]{:S(2)}, u32[]{:S(2)}) %all-to-all-start) | async-done | bytes 98336 | tf_op jit(solution)/shard_map/all_to_all | solution.py:317
  41.0 0.0 copy-done
  41.0 0.5 mix_heads.1
  41.5 18.0 %all_to_all.15 = bf16[48,8,128]{2,1,0:T(8,128)(2,1)S(1)} all-to-all(bf16[48,8,128]{2,1,0:T(8,128)(2,1)S(1)} %mix_heads.1), channel_id=1, replica_groups=mesh['tensor'=48,'context'=16] {'tensor'}, dimensions={0} | all-to-all | bytes 196608 | tf_op jit(solution)/shard_map/all_to_all | solution.py:317
  59.6 1.0 repeat.1
  60.5 4.2 %all-to-all-start.2 = ((bf16[8,384,128]{2,1,0:T(8,128)(2,1)}), bf16[8,384,128]{2,1,0:T(8,128)(2,1)S(1)}, u32[]{:S(2)}, u32[]{:S(2)}) async-start(bf16[8,384,128]{2,1,0:T(8,128)(2,1)} %repeat.1), calls=%async_computation.2 | async-start | bytes 1572864 | tf_op jit(solution)/shard_map/all_to_all | solution.py:320
  64.7 6.1 %project_queries_keys.1 = (bf16[384,128]{1,0:T(8,128)(2,1)}, bf16[1,400,128]{2,1,0:T(8,128)(2,1)S(1)}) custom-call(s32[4]{0:T(128)} %ids_ref.3, bf16[384,8192]{1,0:T(8,128)(2,1)} %x_ref.2, bf16[8192,128]{1,0:T(8,128)(2,1)} %wq_ref.1, bf16[8192,128]{1,0:T(8,128)(2,1)} %wk_ref.1), custom_call_target="tpu_custom_call" | custom-call | tf_op jit(solution)/shard_map/project_queries_keys/pallas_call | solution.py:104
  70.9 3.4 %collective-permute-start = (bf16[1,400,128]{2,1,0:T(8,128)(2,1)S(1)}, bf16[1,400,128]{2,1,0:T(8,128)(2,1)S(1)}, u32[]{:S(2)}, u32[]{:S(2)}) collective-permute-start(bf16[1,400,128]{2,1,0:T(8,128)(2,1)S(1)} %get-tuple-element.14.refs_0_), channel_id=1, source_target_pairs={{0,2},{1,3},{2,0},{3,1},{4,6},{5,7},{6,4},{7,5},{8,10},{9,11},{10,... | collective-permute-start | bytes 307208 | tf_op jit(solution)/shard_map/ppermute | solution.py:325
  74.2 3.2 %collective-permute-done.refs_1_ = bf16[1,400,128]{2,1,0:T(8,128)(2,1)S(1)} collective-permute-done((bf16[1,400,128]{2,1,0:T(8,128)(2,1)S(1)}, bf16[1,400,128]{2,1,0:T(8,128)(2,1)S(1)}, u32[]{:S(2)}, u32[]{:S(2)}) %collective-permute-start) | collective-permute-done | bytes 102432 | tf_op jit(solution)/shard_map/ppermute | solution.py:325
  77.4 2.8 %collective-permute-start.1 = (bf16[2,400,128]{2,1,0:T(8,128)(2,1)S(1)}, bf16[2,400,128]{2,1,0:T(8,128)(2,1)S(1)}, u32[]{:S(2)}, u32[]{:S(2)}) collective-permute-start(bf16[2,400,128]{2,1,0:T(8,128)(2,1)S(1)} %pack.2.refs_0_), channel_id=1, source_target_pairs={{0,4},{1,5},{2,6},{3,7},{4,0},{5,1},{6,2},{7,3},{8,12},{9,13},{10,... | collective-permute-start | bytes 614408 | tf_op jit(solution)/shard_map/ppermute | solution.py:325
  80.3 3.7 %collective-permute-start.2 = (bf16[2,400,128]{2,1,0:T(8,128)(2,1)S(1)}, bf16[2,400,128]{2,1,0:T(8,128)(2,1)S(1)}, u32[]{:S(2)}, u32[]{:S(2)}) collective-permute-start(bf16[2,400,128]{2,1,0:T(8,128)(2,1)S(1)} %pack.2.refs_0_), channel_id=1, source_target_pairs={{0,12},{1,13},{2,14},{3,15},{4,8},{5,9},{6,10},{7,11},{8,4},{9,5},... | collective-permute-start | bytes 614408 | tf_op jit(solution)/shard_map/ppermute | solution.py:325
  83.9 2.6 %collective-permute-start.3 = (bf16[2,400,128]{2,1,0:T(8,128)(2,1)S(1)}, bf16[2,400,128]{2,1,0:T(8,128)(2,1)S(1)}, u32[]{:S(2)}, u32[]{:S(2)}) collective-permute-start(bf16[2,400,128]{2,1,0:T(8,128)(2,1)S(1)} %pack.2.refs_0_), channel_id=1, source_target_pairs={{0,8},{1,9},{2,10},{3,11},{4,12},{5,13},{6,14},{7,15},{8,0},{9,1},... | collective-permute-start | bytes 614408 | tf_op jit(solution)/shard_map/ppermute | solution.py:325
  86.5 0.0 collective-permute-done.1.refs_1_
  86.5 1.5 %collective-permute-done.2.refs_2_ = bf16[2,400,128]{2,1,0:T(8,128)(2,1)S(1)} collective-permute-done((bf16[2,400,128]{2,1,0:T(8,128)(2,1)S(1)}, bf16[2,400,128]{2,1,0:T(8,128)(2,1)S(1)}, u32[]{:S(2)}, u32[]{:S(2)}) %collective-permute-start.2) | collective-permute-done | bytes 204832 | tf_op jit(solution)/shard_map/ppermute | solution.py:325
  88.0 5.2 %collective-permute-done.3.refs_3_ = bf16[2,400,128]{2,1,0:T(8,128)(2,1)S(1)} collective-permute-done((bf16[2,400,128]{2,1,0:T(8,128)(2,1)S(1)}, bf16[2,400,128]{2,1,0:T(8,128)(2,1)S(1)}, u32[]{:S(2)}, u32[]{:S(2)}) %collective-permute-start.3) | collective-permute-done | bytes 204832 | tf_op jit(solution)/shard_map/ppermute | solution.py:325
  93.2 0.1 pack.3.refs_0_
  93.3 7.1 %collective-permute-start.4 = (bf16[8,400,128]{2,1,0:T(8,128)(2,1)S(1)}, bf16[8,400,128]{2,1,0:T(8,128)(2,1)S(1)}, u32[]{:S(2)}, u32[]{:S(2)}) collective-permute-start(bf16[8,400,128]{2,1,0:T(8,128)(2,1)S(1)} %pack.3.refs_0_), channel_id=1, source_target_pairs={{0,1},{1,0},{2,3},{3,2},{4,5},{5,4},{6,7},{7,6},{8,9},{9,8},{10,11... | collective-permute-start | bytes 2457608 | tf_op jit(solution)/shard_map/ppermute | solution.py:325
  100.3 0.0 all-to-all-done.2.v_ref
  100.3 1.9 %collective-permute-start.5 = (bf16[8,384,128]{2,1,0:T(8,128)(2,1)S(1)}, bf16[8,384,128]{2,1,0:T(8,128)(2,1)S(1)}, u32[]{:S(2)}, u32[]{:S(2)}) collective-permute-start(bf16[8,384,128]{2,1,0:T(8,128)(2,1)S(1)} %all-to-all-done.2.v_ref), channel_id=1, source_target_pairs={{0,1},{1,0},{2,3},{3,2},{4,5},{5,4},{6,7},{7,6},{8,9},{9,8},{10,11... | collective-permute-start | bytes 2359304 | tf_op jit(solution)/shard_map/ppermute | solution.py:325
  102.3 0.0 collective-permute-done.4.refs_1_
  102.3 3.5 %attention_weights.1 = (bf16[2,192,3072]{2,1,0:T(8,128)(2,1)S(1)}, f32[384,128]{1,0:T(8,128)}) custom-call(s32[4]{0:T(128)} %ids_ref.3, bf16[384,128]{1,0:T(8,128)(2,1)} %get-tuple-element.13.q_ref, bf16[8,400,128]{2,1,0:T(8,128)(2,1)S(1)} %pack.3.refs_0_, bf16[8,400,128]{2,1,0:T(8,128)(2,1)S(1)} %collective-permute-done.4.refs_1_), custom_call_target="tpu_custom_call" | custom-call | tf_op jit(solution)/shard_map/attention_weights/pallas_call | solution.py:201
  105.8 1.4 %apply_first.1 = (f32[384,128]{1,0:T(8,128)S(1)}, f32[384,128]{1,0:T(8,128)S(1)}) custom-call(bf16[2,192,3072]{2,1,0:T(8,128)(2,1)S(1)} %get-tuple-element.15.w_ref, f32[384,128]{1,0:T(8,128)} %get-tuple-element.16.total_ref, bf16[8,384,128]{2,1,0:T(8,128)(2,1)S(1)} %all-to-all-done.2.v_ref), custom_call_target="tpu_custom_call" | custom-call | tf_op jit(solution)/shard_map/apply_first/pallas_call | solution.py:249
  107.2 0.0 collective-permute-done.5.v_ref
  107.2 1.1 %apply_last.1 = bf16[384,128]{1,0:T(8,128)(2,1)} custom-call(bf16[2,192,3072]{2,1,0:T(8,128)(2,1)S(1)} %get-tuple-element.15.w_ref, f32[384,128]{1,0:T(8,128)S(1)} %get-tuple-element.17.total_ref, f32[384,128]{1,0:T(8,128)S(1)} %get-tuple-element.18.part_ref, bf16[8,384,128]{2,1,0:T(8,128)(2,1)S(1)} %collective-permute-done.5.v_ref), custom_call_target="tpu_custom_call" | custom-call | tf_op jit(solution)/shard_map/apply_last/pallas_call | solution.py:260
  (2 shorter events, 0.0 us)
Async XLA Ops:
  0.0 26.7 %copy-start.1 = (bf16[48,96]{1,0:T(8,128)(2,1)S(1)}, bf16[48,96]{1,0:T(8,128)(2,1)}, u32[]{:S(2)}) copy-start(bf16[48,96]{1,0:T(8,128)(2,1)} %param.13) | copy-start | bytes 27652
  0.0 26.8 %copy-start.2 = (bf16[48,96]{1,0:T(8,128)(2,1)S(1)}, bf16[48,96]{1,0:T(8,128)(2,1)}, u32[]{:S(2)}) copy-start(bf16[48,96]{1,0:T(8,128)(2,1)} %param.12) | copy-start | bytes 27652
  0.0 41.0 %copy-start = (bf16[96,48]{0,1:T(8,128)(2,1)S(1)}, bf16[96,48]{0,1:T(8,128)(2,1)}, u32[]{:S(2)}) copy-start(bf16[96,48]{0,1:T(8,128)(2,1)} %param.14) | copy-start | bytes 27652
  5.1 35.9 %all-to-all-start = ((bf16[48,8,128]{2,1,0:T(8,128)(2,1)}), bf16[48,8,128]{2,1,0:T(8,128)(2,1)S(1)}, u32[]{:S(2)}, u32[]{:S(2)}) async-start(bf16[48,8,128]{2,1,0:T(8,128)(2,1)} %bitcast), calls=%async_computation | async-start | bytes 196608 | tf_op jit(solution)/shard_map/all_to_all | solution.py:317
  60.5 39.8 %all-to-all-start.2 = ((bf16[8,384,128]{2,1,0:T(8,128)(2,1)}), bf16[8,384,128]{2,1,0:T(8,128)(2,1)S(1)}, u32[]{:S(2)}, u32[]{:S(2)}) async-start(bf16[8,384,128]{2,1,0:T(8,128)(2,1)} %repeat.1), calls=%async_computation.2 | async-start | bytes 1572864 | tf_op jit(solution)/shard_map/all_to_all | solution.py:320
  70.9 6.6 %collective-permute-start = (bf16[1,400,128]{2,1,0:T(8,128)(2,1)S(1)}, bf16[1,400,128]{2,1,0:T(8,128)(2,1)S(1)}, u32[]{:S(2)}, u32[]{:S(2)}) collective-permute-start(bf16[1,400,128]{2,1,0:T(8,128)(2,1)S(1)} %get-tuple-element.14.refs_0_), channel_id=1, source_target_pairs={{0,2},{1,3},{2,0},{3,1},{4,6},{5,7},{6,4},{7,5},{8,10},{9,11},{10,... | collective-permute-start | bytes 307208 | tf_op jit(solution)/shard_map/ppermute | solution.py:325
  77.4 9.1 %collective-permute-start.1 = (bf16[2,400,128]{2,1,0:T(8,128)(2,1)S(1)}, bf16[2,400,128]{2,1,0:T(8,128)(2,1)S(1)}, u32[]{:S(2)}, u32[]{:S(2)}) collective-permute-start(bf16[2,400,128]{2,1,0:T(8,128)(2,1)S(1)} %pack.2.refs_0_), channel_id=1, source_target_pairs={{0,4},{1,5},{2,6},{3,7},{4,0},{5,1},{6,2},{7,3},{8,12},{9,13},{10,... | collective-permute-start | bytes 614408 | tf_op jit(solution)/shard_map/ppermute | solution.py:325
  80.3 7.7 %collective-permute-start.2 = (bf16[2,400,128]{2,1,0:T(8,128)(2,1)S(1)}, bf16[2,400,128]{2,1,0:T(8,128)(2,1)S(1)}, u32[]{:S(2)}, u32[]{:S(2)}) collective-permute-start(bf16[2,400,128]{2,1,0:T(8,128)(2,1)S(1)} %pack.2.refs_0_), channel_id=1, source_target_pairs={{0,12},{1,13},{2,14},{3,15},{4,8},{5,9},{6,10},{7,11},{8,4},{9,5},... | collective-permute-start | bytes 614408 | tf_op jit(solution)/shard_map/ppermute | solution.py:325
  83.9 9.3 %collective-permute-start.3 = (bf16[2,400,128]{2,1,0:T(8,128)(2,1)S(1)}, bf16[2,400,128]{2,1,0:T(8,128)(2,1)S(1)}, u32[]{:S(2)}, u32[]{:S(2)}) collective-permute-start(bf16[2,400,128]{2,1,0:T(8,128)(2,1)S(1)} %pack.2.refs_0_), channel_id=1, source_target_pairs={{0,8},{1,9},{2,10},{3,11},{4,12},{5,13},{6,14},{7,15},{8,0},{9,1},... | collective-permute-start | bytes 614408 | tf_op jit(solution)/shard_map/ppermute | solution.py:325
  93.3 9.0 %collective-permute-start.4 = (bf16[8,400,128]{2,1,0:T(8,128)(2,1)S(1)}, bf16[8,400,128]{2,1,0:T(8,128)(2,1)S(1)}, u32[]{:S(2)}, u32[]{:S(2)}) collective-permute-start(bf16[8,400,128]{2,1,0:T(8,128)(2,1)S(1)} %pack.3.refs_0_), channel_id=1, source_target_pairs={{0,1},{1,0},{2,3},{3,2},{4,5},{5,4},{6,7},{7,6},{8,9},{9,8},{10,11... | collective-permute-start | bytes 2457608 | tf_op jit(solution)/shard_map/ppermute | solution.py:325
  100.3 6.9 %collective-permute-start.5 = (bf16[8,384,128]{2,1,0:T(8,128)(2,1)S(1)}, bf16[8,384,128]{2,1,0:T(8,128)(2,1)S(1)}, u32[]{:S(2)}, u32[]{:S(2)}) collective-permute-start(bf16[8,384,128]{2,1,0:T(8,128)(2,1)S(1)} %all-to-all-done.2.v_ref), channel_id=1, source_target_pairs={{0,1},{1,0},{2,3},{3,2},{4,5},{5,4},{6,7},{7,6},{8,9},{9,8},{10,11... | collective-permute-start | bytes 2359304 | tf_op jit(solution)/shard_map/ppermute | solution.py:325
